TPU v7x, 512 devices: a whole 4x8x8 slice. The times are simulated.
512 devices in a mesh: row: 64 (over z, y), col: 8 (over x, core).
Axes of the slice: x: 4, y: 8, z: 8, core: 2. Of those that a mesh axis runs over, the one named last changes fastest.
Arguments:
- matrix: float32 [2, 8192, 16, 1024], P(None, 'row', None, 'col'), may hold values from 0 to 32748, as said below
- pivot_rows: int32 [128], replicated, may hold values from 128 to 16383, as said below
- column_order: int32 [128], replicated, may hold values from 0 to 127, each once
- lower_inverse: int32 [128, 128], replicated, may hold values from 0 to 32748
- upper_inverse: int32 [128, 128], replicated, may hold values from 0 to 32748
Outputs:
- factored: float32 [2, 8192, 16, 1024], P(None, 'row', None, 'col')
Inputs may be any that keep to these rules, and one draw needn't show every extreme that they name: `matrix`: every entry is a whole number. `pivot_rows`: 128 distinct rows, none of them below 128; 128 and 16383 are always among them.
All inputs are finite; a program needn't handle non-finite values.
Results may differ from a plain program's by a relative error of at most 0.0003.
Values sent between devices are 32-bit elements; how exact they have to be, the bound alone decides.
A program may use at most 64 MiB of HBM per device.

v0:
```python
import jax
import jax.numpy as jnp
from jax import lax
from jax.sharding import PartitionSpec as P

prime_modulus = 32749
limb_divisors = (1, 32, 1024)


def broadcast(array, axis, root):
    return lax.dynamic_index_in_dim(lax.all_gather(array, axis), root, 0, keepdims=False)


def split_limbs(values):
    return [(values // divisor % 32).astype(jnp.bfloat16) for divisor in limb_divisors]


def modular_product(left_side, right_side):
    left_limbs = split_limbs(left_side.astype(jnp.int32))
    right_limbs = split_limbs(right_side.astype(jnp.int32))
    outcome = jnp.zeros((left_side.shape[0], right_side.shape[1]), jnp.int32)
    factor = 1
    for degree in range(5):
        limb_pairs = [
            (left_degree, degree - left_degree)
            for left_degree in range(3)
            if 0 <= degree - left_degree < 3
        ]
        stacked_left = jnp.concatenate(
            [left_limbs[limb_pair[0]] for limb_pair in limb_pairs], axis=1
        )
        stacked_right = jnp.concatenate(
            [right_limbs[limb_pair[1]] for limb_pair in limb_pairs], axis=0
        )
        partial_sum = jnp.dot(
            stacked_left, stacked_right, preferred_element_type=jnp.float32
        ).astype(jnp.int32)
        outcome = (outcome + partial_sum % prime_modulus * factor % prime_modulus) % prime_modulus
        factor = factor * 32 % prime_modulus
    return outcome


def on_device(matrix, pivot_rows, column_order, lower_inverse, upper_inverse):
    row_cycles = matrix.shape[0]
    panel_width = matrix.shape[1]
    col_cycles = matrix.shape[2]
    local_rows = row_cycles * panel_width
    local_cols = col_cycles * panel_width
    row_count = lax.axis_size("row")
    row_rank = lax.axis_index("row")
    col_rank = lax.axis_index("col")
    flat = matrix.reshape(local_rows, local_cols)
    stride = row_count * panel_width
    owner = pivot_rows % stride // panel_width
    local_slot = pivot_rows // stride * panel_width + pivot_rows % panel_width
    owned = owner == row_rank
    picked = jnp.where(owned[:, None], flat[jnp.where(owned, local_slot, 0)], 0.0)
    top_rows = jnp.where(row_rank == 0, flat[:panel_width], 0.0)
    new_top, old_top = lax.psum((picked, top_rows), "row")
    upper_all = modular_product(lower_inverse, new_top)
    targets = jnp.where(owned, local_slot, local_rows)
    swapped = flat.at[targets].set(old_top, mode="drop")
    panel = swapped[:, :panel_width][:, column_order]
    panel_all = broadcast(panel, "col", 0)
    lower_all = modular_product(panel_all, upper_inverse)
    permuted = upper_all.at[:, :panel_width].set(upper_all[:, column_order])
    upper_use = jnp.where(col_rank == 0, permuted, upper_all)
    update = modular_product(lower_all, upper_use)
    result = (swapped.astype(jnp.int32) - update) % prime_modulus
    result = result.at[:, :panel_width].set(
        jnp.where(col_rank == 0, lower_all, result[:, :panel_width])
    )
    result = result.at[:panel_width].set(jnp.where(row_rank == 0, upper_use, result[:panel_width]))
    return result.astype(jnp.float32).reshape(row_cycles, panel_width, col_cycles, panel_width)


def solution(mesh):
    return jax.shard_map(
        on_device,
        mesh=mesh,
        in_specs=(P(None, "row", None, "col"), P(), P(), P(), P()),
        out_specs=P(None, "row", None, "col"),
        check_vma=False,
    )
```

profile of v0, /device:TPU:1, one launch (start us, length us, event | category | flops | bytes accessed | tf_op | source)
XLA Modules:
  0.0 259.3 jit_solution(16525342599639331926)
XLA Ops:
  6.5 0.7 compare_select_fusion.1
  7.2 0.0 copy-start
  7.3 1.4 slice_select_fusion.1
  8.7 1.3 copy.50
  10.0 0.9 copy.49
  10.9 1.0 gather_fusion.1
  11.9 1.3 copy.23
  13.2 2.3 broadcast_select_fusion
  15.5 0.0 all-reduce.3.cloned.1.call-update
  15.5 0.0 all-gather.3.cloned.1.call-start
  15.6 0.7 compare_reduce_fusion
  16.3 0.1 fusion.165
  16.4 0.1 fusion.159
  16.6 164.6 %all-reduce.3.cloned.1.call-done = (f32[128,2048]{1,0:T(8,128)}, f32[128,2048]{0,1:T(8,128)}) async-done(((f32[128,2048]{1,0:T(8,128)}, f32[128,2048]{0,1:T(8,128)}), (f32[128,2048]{1,0:T(8,128)}, f32[128,2048]{0,1:T(8,128)})) %all-reduce.3.cloned.1.call-update) | async-done | bytes 2097168 | tf_op jit(solution)/shard_map/psum | solution.py:59
  181.2 2.7 %scatter_fusion = f32[256,2048]{1,0:T(8,128)S(1)} fusion(f32[256,2048]{1,0:T(8,128)S(1)} %bitcast.29, s32[128]{0:T(128)S(1)} %compare_select_fusion.3, f32[128,2048]{1,0:T(8,128)} %get-tuple-element.41), kind=kCustom, calls=%fused_computation.3 | custom fusion | bytes 3146240 | tf_op jit(solution)/shard_map/scatter | solution.py:62
  183.9 1.8 copy.21
  185.7 0.1 copy.22
  185.8 1.4 gather_fusion
  187.2 0.0 all-gather.3.cloned.1.call-update
  187.2 2.3 fusion.45
  189.6 0.7 fusion.7
  190.2 0.7 fusion.8
  190.9 0.9 fusion.6
  191.8 0.7 fusion.9
  192.4 8.6 %add_select_fusion.21 = s32[128,2048]{0,1:T(8,128)S(1)} fusion(bf16[128,128]{1,0:T(8,128)(2,1)S(1)} %get-tuple-element.64, bf16[128,2048]{0,1:T(8,128)(2,1)S(1)} %get-tuple-element.54, s32[128,2048]{0,1:T(8,128)S(1)} %fusion.9, s32[128,2048]{0,1:T(8,128)S(1)} %fusion.6, s32[128,2048]{0,1:T(8,128)S(1)} %fusion.8, s32[128,2048]{0,1:T(8,128)S(1)} %fusion.7), kind=kOutput, calls=%fused_computation.85 | convolution fusion | flops 92012544 | bytes 5799936 | tf_op jit(solution)/shard_map/dot_general | solution.py:35
  201.0 0.6 gather_fusion.2
  201.7 0.6 fusion.171
  202.3 2.2 fusion.69
  204.6 12.3 %all-gather.3.cloned.1.call-done = f32[2048,128]{0,1:T(8,128)} async-done(((f32[256,128]{0,1:T(8,128)}), f32[2048,128]{0,1:T(8,128)}) %all-gather.3.cloned.1.call-update) | async-done | bytes 1048592 | tf_op jit(solution)/shard_map/all_gather | solution.py:11
  216.8 1.0 fusion.102
  217.8 1.1 fusion.108
  218.9 1.0 fusion.115
  219.9 0.3 fusion.40
  220.2 0.3 fusion.42
  220.5 0.3 fusion.41
  220.7 0.3 fusion.43
  221.0 1.3 fusion.126
  222.3 1.2 fusion.3
  223.5 1.2 fusion
  224.8 1.2 fusion.4
  226.0 1.4 fusion.1
  227.3 0.2 copy-done.1
  227.6 18.9 %add_select_fusion = s32[256,2048]{0,1:T(8,128)S(1)} fusion(f32[256,2048]{0,1:T(8,128)S(1)} %copy-done.1, s32[256,2048]{0,1:T(8,128)S(1)} %fusion.4, s32[256,2048]{0,1:T(8,128)S(1)} %fusion, s32[256,2048]{0,1:T(8,128)S(1)} %fusion.3, s32[256,2048]{0,1:T(8,128)S(1)} %fusion.1, bf16[128,2048]{0,1:T(8,128)(2,1)S(1)} %get-tuple-element.51, ...), kind=kOutput, calls=%fused_computation.4 | convolution fusion | flops 188219392 | bytes 13172736 | tf_op jit(solution)/shard_map/dot_general | solution.py:35
  246.5 0.7 fusion.132
  247.2 0.2 fusion.75
  247.4 0.1 convert_element_type.151
  247.5 2.1 reshape.85
  249.6 2.9 %copy.34 = f32[2,128,16,128]{3,2,1,0:T(8,128)} copy(f32[2,128,16,128]{1,0,3,2:T(2,128)} %reshape.85) | data formatting | bytes 4194304 | tf_op jit(solution)/shard_map/reshape | solution.py:74
  (14 shorter events, 0.1 us)
Async XLA Ops:
  6.5 174.6 %all-reduce.3.cloned.1.call-start = ((), (), s32[]{:S(2)}) async-start(), calls=%async_computation.1 | async-start | bytes 4194304 | tf_op jit(solution)/shard_map/psum | solution.py:59
  7.2 2.8 %copy-start = (f32[2,128,16,128]{3,2,1,0:T(8,128)S(1)}, f32[2,128,16,128]{3,2,1,0:T(8,128)}, u32[]{:S(2)}) copy-start(f32[2,128,16,128]{3,2,1,0:T(8,128)} %param.11) | copy-start | bytes 6291460
  13.2 3.1 %copy-start.3 = (s32[128,128]{1,0:T(8,128)S(1)}, s32[128,128]{1,0:T(8,128)}, u32[]{:S(2)}) copy-start(s32[128,128]{1,0:T(8,128)} %param.14) | copy-start | bytes 196612
  13.2 3.2 %copy-start.4 = (s32[128,128]{1,0:T(8,128)S(1)}, s32[128,128]{1,0:T(8,128)}, u32[]{:S(2)}) copy-start(s32[128,128]{1,0:T(8,128)} %param.15) | copy-start | bytes 196612
  15.5 201.3 %all-gather.3.cloned.1.call-start = ((), (), s32[]{:S(2)}) async-start(), calls=%async_computation | async-start | bytes 1179648 | tf_op jit(solution)/shard_map/all_gather | solution.py:11
  183.9 3.3 %copy-start.2 = (f32[128,2048]{0,1:T(8,128)S(1)}, f32[128,2048]{0,1:T(8,128)}, u32[]{:S(2)}) copy-start(f32[128,2048]{0,1:T(8,128)} %get-tuple-element.42) | copy-start | bytes 3145732
  226.0 1.6 copy-start.1
Sparse Core Ops, SparseCore 0:
  15.6 165.4 all-reduce.2
  187.4 29.4 all-gather.2
where the time goes:
time: 260 us; the launch traced here: 259 us
  waiting for transfers between devices  177 us (68%)
  matrix products  37.7 us (15%)
  local copies, waits for them, and re-layouts  16.3 us (6%)
  other arithmetic  14.6 us (6%)
  between operations  13.7 us (5%)
    psum x1, waiting for transfers between devices, on_device(): new_top, old_top = lax.psum((picked, top_rows), 'row')  165 us
    dot_general x15, matrix products, modular_product(): jnp.dot(stacked_left, stacked_right, preferred_element_type=jnp.float32)  37.7 us
    all_gather x1, waiting for transfers between devices, broadcast(): lax.all_gather(array, axis)  12.3 us
    convert_element_type x7, other arithmetic, split_limbs(): (values // divisor % 32).astype(jnp.bfloat16)  7.92 us
  transfers between devices with their start and end apart: 2, of which 2 were waited for; matrix products, arithmetic and copies ran while one was open for 7% of the time, Pallas kernels for 0%

commit v1 on v0

--- a/solution.py
+++ b/solution.py
@@ -1,14 +1,27 @@
 import jax
 import jax.numpy as jnp
 from jax import lax
+from jax.experimental import pallas as pl
+from jax.experimental.pallas import tpu as pltpu
 from jax.sharding import PartitionSpec as P
 
 prime_modulus = 32749
 limb_divisors = (1, 32, 1024)
-
-
-def broadcast(array, axis, root):
-    return lax.dynamic_index_in_dim(lax.all_gather(array, axis), root, 0, keepdims=False)
+PF = 32749.0
+INV = 1.0 / 32749.0
+MESH = pl.DeviceIdType.MESH
+F32 = jnp.float32
+BF16 = jnp.bfloat16
+I32 = jnp.int32
+
+
+def sum_over(array, axis):
+    count = lax.axis_size(axis)
+    step = 1
+    while step < count:
+        array = array + lax.ppermute(array, axis, [(i, i ^ step) for i in range(count)])
+        step *= 2
+    return array
 
 
 def split_limbs(values):
@@ -40,7 +53,7 @@
     return outcome
 
 
-def on_device(matrix, pivot_rows, column_order, lower_inverse, upper_inverse):
+def general_path(matrix, pivot_rows, column_order, lower_inverse, upper_inverse):
     row_cycles = matrix.shape[0]
     panel_width = matrix.shape[1]
     col_cycles = matrix.shape[2]
@@ -56,12 +69,12 @@
     owned = owner == row_rank
     picked = jnp.where(owned[:, None], flat[jnp.where(owned, local_slot, 0)], 0.0)
     top_rows = jnp.where(row_rank == 0, flat[:panel_width], 0.0)
-    new_top, old_top = lax.psum((picked, top_rows), "row")
+    new_top, old_top = sum_over(picked, "row"), sum_over(top_rows, "row")
     upper_all = modular_product(lower_inverse, new_top)
     targets = jnp.where(owned, local_slot, local_rows)
     swapped = flat.at[targets].set(old_top, mode="drop")
     panel = swapped[:, :panel_width][:, column_order]
-    panel_all = broadcast(panel, "col", 0)
+    panel_all = sum_over(jnp.where(col_rank == 0, panel, 0.0), "col")
     lower_all = modular_product(panel_all, upper_inverse)
     permuted = upper_all.at[:, :panel_width].set(upper_all[:, column_order])
     upper_use = jnp.where(col_rank == 0, permuted, upper_all)
@@ -74,6 +87,519 @@
     return result.astype(jnp.float32).reshape(row_cycles, panel_width, col_cycles, panel_width)
 
 
+R_T1, R_T2, R_T3, R_O1, R_O2, R_O3, R_TV, R_OK = 0, 2, 4, 6, 8, 10, 12, 14
+
+
+def table_kernel(rank_ref, pivots_ref, out_ref):
+    me = rank_ref[0]
+    my_z, my_y = me >> 3, me & 7
+    sub = lax.broadcasted_iota(I32, (128, 128), 0)
+    lane = lax.broadcasted_iota(I32, (128, 128), 1)
+    eye = sub == lane
+    t = lax.broadcasted_iota(I32, (1, 128), 1)
+    pivots = pivots_ref[...]
+
+    def column(row):
+        return jnp.sum(jnp.where(eye, row.astype(F32), 0.0), axis=1, keepdims=True)
+
+    owner = (pivots & 8191) >> 7
+    slot_col = column(((pivots >> 13) << 7) | (pivots & 127))
+    index_col = lax.broadcasted_iota(I32, (128, 1), 0).astype(F32)
+    good = jnp.ones((1, 128), jnp.bool_)
+    out_ref[...] = jnp.zeros_like(out_ref)
+    for c in range(2):
+        if c == 0:
+            key, plane, minor = owner, my_z, my_y
+        else:
+            key, plane, minor = ((owner & 7) << 3) | (owner >> 3), my_y, my_z
+        key_col = column(key)
+        full_row = (key * 128 + t).astype(F32)
+        full_col = key_col * 128.0 + index_col
+        rank_col = jnp.sum(jnp.where(full_row < full_col, 1.0, 0.0), axis=1, keepdims=True)
+
+        def before(x):
+            return jnp.sum(
+                jnp.where(key_col < x.astype(F32), 1.0, 0.0), axis=0, keepdims=True
+            ).astype(I32)
+
+        def at_rank(values_col, s):
+            return jnp.sum(
+                jnp.where(rank_col == s.astype(F32), values_col, 0.0), axis=0, keepdims=True
+            ).astype(I32)
+
+        def first(start, residue):
+            return start + ((residue - start) & 7)
+
+        zero = jnp.zeros((1, 128), I32)
+        half, odd = t >> 1, t & 1
+        mine = zero + (plane * 8 + minor)
+        start = before(mine)
+        end = before(mine + 1)
+        s = first(start, half) + 8 * odd
+        slot = at_rank(slot_col, s)
+        held = (s < end) & (t < 16)
+        out_ref[R_T1 + c:R_T1 + c + 1, :] = jnp.where(held, slot, 0)
+        out_ref[R_TV + c:R_TV + c + 1, :] = jnp.where(held, slot, -1)
+
+        plane_start = before(zero + plane * 8)
+        my_first = first(plane_start, minor)
+        s = my_first + 8 * t
+        key_s = at_rank(key_col, s)
+        start = before(key_s)
+        where_n2 = (key_s & 7) * 2 + ((s - first(start, minor)) >> 3)
+        out_ref[R_T2 + c:R_T2 + c + 1, :] = jnp.clip(where_n2, 0, 15)
+
+        s = 8 * t + minor
+        plane_s = at_rank(key_col, s) >> 3
+        place = plane_s * 4 + ((s - first(before(plane_s * 8), minor)) >> 3)
+        out_ref[R_T3 + c:R_T3 + c + 1, :] = jnp.clip(place, 0, 31)
+
+        s = 8 * (t & 15) + (t >> 4)
+        out_ref[R_O1 + c:R_O1 + c + 1, :] = at_rank(index_col, s)
+
+        s = first(before((t >> 2) * 8), minor) + 8 * (t & 3)
+        out_ref[R_O2 + c:R_O2 + c + 1, :] = jnp.clip((s - minor) >> 3, 0, 15)
+
+        s = first(before(zero + plane * 8 + half), minor) + 8 * odd
+        out_ref[R_O3 + c:R_O3 + c + 1, :] = jnp.clip((s - my_first) >> 3, 0, 3)
+
+        if c == 0:
+            good = good & (before(t + 1) - before(t) <= 16)
+        good = good & (before(t * 8 + 8) - before(t * 8) <= 32)
+    worst = jnp.min(jnp.where(good, 1.0, 0.0), axis=1, keepdims=True)
+    out_ref[R_OK:R_OK + 1, :] = jnp.broadcast_to(worst, (1, 128)).astype(I32)
+
+
+def make_tables(row_rank, pivot_rows):
+    return pl.pallas_call(
+        table_kernel,
+        name="tables",
+        out_shape=jax.ShapeDtypeStruct((16, 128), I32),
+        in_specs=[
+            pl.BlockSpec(memory_space=pltpu.SMEM),
+            pl.BlockSpec(memory_space=pltpu.VMEM),
+        ],
+        out_specs=pl.BlockSpec(memory_space=pltpu.VMEM),
+    )(row_rank.reshape(1), pivot_rows.reshape(1, 128))
+
+
+def exchange_kernel(
+    tab, mat, new_out, old_out, pan_out, opan_out,
+    n1s, n1r, n2s, n2r, o1s, o1r, o2s, o2r, o3s,
+    n1_ss, n1_rs, n2_ss, n2_rs, n3_ss, n3_rs, o1_ss, o1_rs, o2_ss, o2_rs, o3_ss, o3_rs,
+    p1_ss, p1_rs, p2_ss, p2_rs,
+):
+    rank = lax.axis_index("row")
+    col = lax.axis_index("col")
+    z, y = rank // 8, rank % 8
+    coords = ((z, y), (y, z))
+
+    def row_of(c, plane, minor):
+        return plane * 8 + minor if c == 0 else minor * 8 + plane
+
+    def minor_peer(c, step):
+        plane, minor = coords[c]
+        other = (minor + step) % 8
+        return other, (row_of(c, plane, other), col)
+
+    def plane_peer(c, step):
+        plane, minor = coords[c]
+        other = (plane + step) % 8
+        return other, (row_of(c, other, minor), col)
+
+    def col_peer(step):
+        return (rank, (col + step) % 8)
+
+    def copy(src, dst, ssem, rsem, dev):
+        return pltpu.make_async_remote_copy(
+            src_ref=src, dst_ref=dst, send_sem=ssem, recv_sem=rsem,
+            device_id=dev, device_id_type=MESH,
+        )
+
+    new2d = new_out.reshape(2 * 8 * 128, 128)
+
+    barrier = pltpu.get_barrier_semaphore()
+    for step in range(1, 8):
+        for dev in (minor_peer(0, step)[1], minor_peer(1, step)[1], col_peer(step)):
+            pl.semaphore_signal(barrier, inc=1, device_id=dev, device_id_type=MESH)
+
+    def mat_tile(row, c):
+        return mat[row * 2 + c]
+
+    for c in range(2):
+        for k in range(16):
+            n1s[c, k] = mat_tile(tab[R_T1 + c, k], c)
+
+    @pl.when(col == 0)
+    def _():
+        pan_out[...] = mat.reshape(4096, 128)[pl.ds(0, 256, stride=16), :]
+
+    @pl.when(rank == 0)
+    def _():
+        for c in range(2):
+            def body(u, carry):
+                o1s[c, u] = mat_tile(tab[R_O1 + c, u], c)
+                return carry
+            lax.fori_loop(0, 128, body, 0)
+
+    pl.semaphore_wait(barrier, 21)
+
+    n1 = []
+    for step in range(1, 8):
+        for c in range(2):
+            other, dev = minor_peer(c, step)
+            minor = coords[c][1]
+            d = copy(n1s.at[c, pl.ds(2 * other, 2)], n1r.at[c, pl.ds(2 * minor, 2)],
+                     n1_ss.at[c, step], n1_rs.at[c, step], dev)
+            d.start()
+            n1.append(d)
+
+    p1 = []
+    for step in range(1, 8):
+        p1.append(copy(pan_out, pan_out, p1_ss.at[step], p1_rs, (rank, step)))
+
+    @pl.when(col == 0)
+    def _():
+        for d in p1:
+            d.start()
+
+    o1 = []
+    for step in (1, 7, 2, 6, 3, 5, 4):
+        for c in range(2):
+            dev = (step if c == 0 else step * 8, col)
+            o1.append(copy(o1s.at[c, pl.ds(16 * step, 16)], o1r.at[c],
+                           o1_ss.at[c, step], o1_rs.at[c], dev))
+
+    @pl.when(rank == 0)
+    def _():
+        for d in o1:
+            d.start()
+        for c in range(2):
+            o1r[c] = o1s[c, pl.ds(0, 16)]
+
+    for c in range(2):
+        minor = coords[c][1]
+        n1r[c, pl.ds(2 * minor, 2)] = n1s[c, pl.ds(2 * minor, 2)]
+
+    for d in n1:
+        d.wait_recv()
+
+    n2 = []
+    for c in range(2):
+        plane = coords[c][0]
+        for j in range(4):
+            row = n1r[c, tab[R_T2 + c, j]]
+            n2s[c, j] = row
+            n2r[c, plane * 4 + j] = row
+    for step in range(1, 8):
+        for c in range(2):
+            plane = coords[c][0]
+            other, dev = plane_peer(c, step)
+            d = copy(n2s.at[c], n2r.at[c, pl.ds(4 * plane, 4)],
+                     n2_ss.at[c, step], n2_rs.at[c, step], dev)
+            d.start()
+            n2.append(d)
+
+    o2 = [[], []]
+    for c in range(2):
+        plane, minor = coords[c]
+        for step in (1, 7, 2, 6, 3, 5, 4):
+            dev = (row_of(c, step, minor), col)
+            o2[c].append(copy(o2s.at[c, pl.ds(4 * step, 4)], o2r.at[c],
+                              o2_ss.at[c, step], o2_rs.at[c], dev))
+
+    def do_o2():
+        for c in range(2):
+            plane, minor = coords[c]
+
+            @pl.when((plane == 0) & (minor != 0))
+            def _():
+                copy(o1s.at[c, pl.ds(0, 16)], o1r.at[c], o1_ss.at[c, 0], o1_rs.at[c],
+                     (0, col)).wait_recv()
+
+            @pl.when(plane == 0)
+            def _():
+                def body(v, carry):
+                    o2s[c, v] = o1r[c, tab[R_O2 + c, v]]
+                    return carry
+                lax.fori_loop(0, 32, body, 0)
+                for d in o2[c]:
+                    d.start()
+                o2r[c] = o2s[c, pl.ds(0, 4)]
+
+    for d in n2:
+        d.wait_recv()
+
+    for c in range(2):
+        minor = coords[c][1]
+        for k in range(16):
+            row = n2r[c, tab[R_T3 + c, k]]
+            new2d[pl.ds(c * 1024 + minor * 16 + k, 8, stride=128), :] = row
+
+    sends = []
+
+    def hop_copies(h):
+        found = []
+        for q in range(2):
+            for c in range(2):
+                minor = coords[c][1]
+                for way in range(2):
+                    if h == 4 and q != way:
+                        continue
+                    sign = 1 if way == 0 else -1
+                    block = (minor - sign * (h - 1)) % 8
+                    part = new_out.at[c, pl.ds(4 * q, 4), pl.ds(pl.multiple_of(16 * block, 16), 16), :]
+                    found.append(copy(part, part, n3_ss.at[c, h, way, q], n3_rs.at[c, h, way, q],
+                                      minor_peer(c, sign)[1]))
+        return found
+
+    hops = {h: hop_copies(h) for h in range(1, 5)}
+
+    def key(h):
+        return [(q, c, way) for q in range(2) for c in range(2) for way in range(2)
+                if not (h == 4 and q != way)]
+
+    for d in hops[1]:
+        d.start()
+    do_o2()
+    for h in range(2, 5):
+        before = dict(zip(key(h - 1), hops[h - 1]))
+        now = dict(zip(key(h), hops[h]))
+        for k in key(h - 1):
+            before[k].wait_recv()
+            if k in now:
+                now[k].start()
+        if h == 2:
+            o3 = []
+            for c in range(2):
+                @pl.when(coords[c][0] != 0)
+                def _():
+                    o2[c][0].wait_recv()
+
+            for c in range(2):
+                minor = coords[c][1]
+                for k in range(16):
+                    o3s[c, k] = o2r[c, tab[R_O3 + c, k]]
+                old_out[c, pl.ds(2 * minor, 2)] = o3s[c, pl.ds(2 * minor, 2)]
+                for step in range(1, 8):
+                    other, dev = minor_peer(c, step)
+                    d = copy(o3s.at[c, pl.ds(2 * other, 2)], old_out.at[c, pl.ds(2 * minor, 2)],
+                             o3_ss.at[c, step], o3_rs.at[c, step], dev)
+                    d.start()
+                    o3.append(d)
+    for d in o3:
+        d.wait_recv()
+    p2 = []
+    for step in range(1, 8):
+        p2.append(copy(opan_out, opan_out, p2_ss.at[step], p2_rs, (rank, step)))
+
+    @pl.when(col == 0)
+    def _():
+        for k in range(16):
+            opan_out[k:k + 1, :] = old_out[0, k, 0:1, :]
+        for d in p2:
+            d.start()
+
+    for d in hops[4]:
+        d.wait_recv()
+
+    @pl.when(col != 0)
+    def _():
+        p1[0].wait_recv()
+        p2[0].wait_recv()
+
+    for d in n1 + n2 + o3 + [d for h in hops for d in hops[h]]:
+        d.wait_send()
+
+    @pl.when(rank == 0)
+    def _():
+        for d in o1:
+            d.wait_send()
+
+    for c in range(2):
+        @pl.when(coords[c][0] == 0)
+        def _():
+            for d in o2[c]:
+                d.wait_send()
+
+    @pl.when(col == 0)
+    def _():
+        for d in p1 + p2:
+            d.wait_send()
+
+
+def exchange(tables, mat):
+    vmem = pl.BlockSpec(memory_space=pltpu.VMEM)
+    dma = pltpu.SemaphoreType.DMA
+    tile = lambda *lead: pltpu.VMEM((*lead, 8, 128), F32)
+    return pl.pallas_call(
+        exchange_kernel,
+        name="exchange",
+        out_shape=(
+            jax.ShapeDtypeStruct((2, 8, 128, 128), F32),
+            jax.ShapeDtypeStruct((2, 16, 8, 128), F32),
+            jax.ShapeDtypeStruct((256, 128), F32),
+            jax.ShapeDtypeStruct((16, 128), F32),
+        ),
+        in_specs=[pl.BlockSpec(memory_space=pltpu.SMEM), vmem],
+        out_specs=(vmem,) * 4,
+        scratch_shapes=[
+            tile(2, 16), tile(2, 16), tile(2, 4), tile(2, 32), tile(2, 128), tile(2, 16),
+            tile(2, 32), tile(2, 4), tile(2, 16),
+            dma((2, 8)), dma((2, 8)), dma((2, 8)), dma((2, 8)),
+            dma((2, 5, 2, 2)), dma((2, 5, 2, 2)),
+            dma((2, 8)), dma((2,)), dma((2, 8)), dma((2,)), dma((2, 8)), dma((2, 8)),
+            dma((8,)), dma, dma((8,)), dma,
+        ],
+        compiler_params=pltpu.CompilerParams(collective_id=0, has_side_effects=True),
+    )(tables, mat)
+
+
+def centred(x):
+    return x - PF * jnp.floor(x * INV + 0.5)
+
+
+def scaled_digits(a):
+    a = centred(a)
+    b = centred(a * 256.0)
+    both = jnp.concatenate([b, a], axis=1)
+    high = jnp.floor(both * (1.0 / 128.0) + 0.5)
+    return jnp.concatenate([high, both - 128.0 * high], axis=0).astype(BF16)
+
+
+def plain_digits(x):
+    high = jnp.floor(x * (1.0 / 256.0) + 0.5)
+    return jnp.concatenate([high.astype(BF16), (x - 256.0 * high).astype(BF16)], axis=0)
+
+
+def product(left, right):
+    both = jnp.dot(left, right, preferred_element_type=F32)
+    rows = both.shape[0] // 2
+    return centred(both[:rows]) * 128.0 + both[rows:]
+
+
+def one_hot_columns(values, hot):
+    high = jnp.floor(values * (1.0 / 256.0))
+    low = values - 256.0 * high
+    return 256.0 * jnp.dot(high.astype(BF16), hot, preferred_element_type=F32) + jnp.dot(
+        low.astype(BF16), hot, preferred_element_type=F32
+    )
+
+
+def compute_kernel(
+    tab, tabv, new_ref, old_ref, pan_ref, opan_ref, order_ref, linv_ref, uinv_ref, mat_hbm,
+    out_ref, mat, pan, low, linv_d, low_d, sem,
+):
+    rank, col = lax.axis_index("row"), lax.axis_index("col")
+    fetch = pltpu.make_async_copy(mat_hbm, mat, sem)
+    fetch.start()
+    sub = lax.broadcasted_iota(I32, (128, 128), 0)
+    eye = sub == lax.broadcasted_iota(I32, (128, 128), 1)
+
+    pan[...] = pan_ref[...]
+
+    def patch_panel(k, carry):
+        slot = tab[R_TV, k]
+
+        @pl.when(slot >= 0)
+        def _():
+            pan[pl.ds(slot, 1), :] = opan_ref[pl.ds(k, 1), :]
+        return carry
+    lax.fori_loop(0, 16, patch_panel, 0)
+
+    order_hot = (sub == order_ref[...]).astype(BF16)
+    uinv = uinv_ref[...].astype(F32)
+    u_high = jnp.floor(uinv * (1.0 / 256.0))
+    u_low = uinv - 256.0 * u_high
+    uperm = 256.0 * jnp.dot(order_hot, u_high.astype(BF16), preferred_element_type=F32) + jnp.dot(
+        order_hot, u_low.astype(BF16), preferred_element_type=F32
+    )
+    lower = centred(product(scaled_digits(pan[...]), plain_digits(centred(uperm))))
+    low[...] = jnp.where(lower < 0.0, lower + PF, lower)
+    top = jnp.where(rank == 0, jnp.where(eye, -1.0, 0.0), lower[:128])
+    low_d[...] = scaled_digits(jnp.concatenate([top, lower[128:]], axis=0))
+
+    linv = linv_ref[...].astype(F32)
+    for c in range(2):
+        hot = (sub == tabv[R_O1 + c:R_O1 + c + 1, :]).astype(BF16)
+        linv_d[c] = scaled_digits(one_hot_columns(linv, hot))
+
+    fetch.wait()
+
+    def patch_rows(k, carry):
+        for c in range(2):
+            slot = tab[R_TV + c, k]
+
+            @pl.when(slot >= 0)
+            def _():
+                mat[pl.ds(pl.multiple_of(slot * 16 + 8 * c, 8), 8), :] = old_ref[c, k]
+        return carry
+    lax.fori_loop(0, 16, patch_rows, 0)
+
+    @pl.when(rank == 0)
+    def _():
+        mat[0:2048, :] = jnp.zeros((2048, 128), F32)
+
+    first_upper = None
+    for pair in range(8):
+        c, e = pair // 4, (pair % 4) * 2
+        x = jnp.concatenate([new_ref[c, e], new_ref[c, e + 1]], axis=1)
+        upper = centred(product(linv_d[c], plain_digits(x)))
+        if pair == 0:
+            first_upper = upper[:, :128]
+        update = product(low_d[...], plain_digits(upper))
+        for side in range(2):
+            rows = pl.ds(2 * pair + side, 256, stride=16)
+            value = mat[rows, :] - update[:, 128 * side:128 * side + 128]
+            out_ref[rows, :] = value - PF * jnp.floor((value + 0.5) * INV)
+
+    @pl.when(col == 0)
+    def _():
+        out_ref[pl.ds(0, 256, stride=16), :] = low[...]
+
+        @pl.when(rank == 0)
+        def _():
+            upper = jnp.where(first_upper < 0.0, first_upper + PF, first_upper)
+            out_ref[pl.ds(0, 128, stride=16), :] = one_hot_columns(upper, order_hot)
+
+
+def compute(tables, new, old, panel, old_panel, column_order, linv, uinv, mat):
+    vmem = pl.BlockSpec(memory_space=pltpu.VMEM)
+    smem = pl.BlockSpec(memory_space=pltpu.SMEM)
+    return pl.pallas_call(
+        compute_kernel,
+        name="update",
+        out_shape=jax.ShapeDtypeStruct((4096, 128), F32),
+        in_specs=[smem] + [vmem] * 8 + [pl.BlockSpec(memory_space=pl.ANY)],
+        out_specs=vmem,
+        scratch_shapes=[
+            pltpu.VMEM((4096, 128), F32),
+            pltpu.VMEM((256, 128), F32),
+            pltpu.VMEM((256, 128), F32),
+            pltpu.VMEM((2, 256, 256), BF16),
+            pltpu.VMEM((512, 256), BF16),
+            pltpu.SemaphoreType.DMA,
+        ],
+    )(tables, tables, new, old, panel, old_panel, column_order, linv, uinv, mat)
+
+
+def fast_path(tables, matrix, column_order, lower_inverse, upper_inverse):
+    mat = matrix.reshape(4096, 128)
+    new, old, panel, old_panel = exchange(tables, matrix.reshape(512, 8, 128))
+    out = compute(tables, new, old, panel, old_panel, column_order.reshape(1, 128),
+                  lower_inverse, upper_inverse, mat)
+    return out.reshape(matrix.shape)
+
+
+def on_device(matrix, pivot_rows, column_order, lower_inverse, upper_inverse):
+    tables = make_tables(lax.axis_index("row"), pivot_rows)
+    return lax.cond(
+        tables[R_OK, 0] > 0,
+        lambda: fast_path(tables, matrix, column_order, lower_inverse, upper_inverse),
+        lambda: general_path(matrix, pivot_rows, column_order, lower_inverse, upper_inverse),
+    )
+
+
 def solution(mesh):
     return jax.shard_map(
         on_device,

time: 260 us -> 54.7 us (0.21)
  the two profiles are of different devices: /device:TPU:1 before, /device:TPU:5 now
where the time goes in v1:
time: 54.7 us; the launch traced here: 54.5 us
  Pallas kernels  52.9 us (97%)
  between operations  0.84 us (2%)
    pallas_call x1, Pallas kernels, exchange(): pl.pallas_call(exchange_kernel, name='exchange', out_shape=(jax.ShapeDtyp...  44.6 us
    pallas_call x1, Pallas kernels, compute(): pl.pallas_call(compute_kernel, name='update', out_shape=jax.ShapeDtypeStr...  7.29 us

profile of v1, /device:TPU:5, one launch (start us, length us, event | category | flops | bytes accessed | tf_op | source)
XLA Modules:
  0.0 54.5 jit_solution(537450065786408406)
XLA Ops:
  0.0 1.0 %tables.1 = s32[16,128]{1,0:T(8,128)S(1)} custom-call(s32[1]{0:T(128)} %bitcast.6.rank_ref, s32[1,128]{1,0:T(1,128)} %bitcast.49), custom_call_target="tpu_custom_call" | custom-call | tf_op jit(solution)/shard_map/tables/pallas_call | solution.py:174
  1.0 0.5 slice.80
  2.2 52.2 %conditional.1 = (f32[2,128,16,128]{3,2,1,0:T(8,128)}) conditional(s32[]{:T(128)} %bitcast.8, (f32[2,128,16,128]{3,2,1,0:T(8,128)}, s32[128]{0:T(128)}, s32[128]{0:T(128)}, s32[128,128]{1,0:T(8,128)}, s32[128,128]{1,0:T(8,128)}) %tuple.23, (f32[2,128,16,128]{3,2,1,0:T(8,128)}, s32[16,128]{1,0:T(8,128)S(1)}, s32[128]{0:T(128)}, s32[128,128]{1,0:T(8,128)}, ...), branch_computations={%region_0.3_spmd, %region_3.4_spmd} | conditional | flops 2036082944 | bytes 204689824 | solution.py:596
  2.4 0.0 copy-start
  2.4 0.0 copy-start.10
  2.4 44.6 %exchange.1 = (f32[2,8,128,128]{3,2,1,0:T(8,128)}, f32[2,16,8,128]{3,2,1,0:T(8,128)}, f32[256,128]{1,0:T(8,128)}, f32[16,128]{1,0:T(8,128)}) custom-call(s32[16,128]{1,0:T(8,128)S(1)} %get-tuple-element.69.tab.tabv, f32[512,8,128]{2,1,0:T(8,128)} %bitcast.43), custom_call_target="tpu_custom_call" | custom-call | tf_op jit(solution)/shard_map/cond/branch_1_fun/exchange/pallas_call | solution.py:435
  47.0 0.0 copy-done
  47.0 0.0 copy-done.10
  47.0 7.3 %update.1 = f32[4096,128]{1,0:T(8,128)} custom-call(s32[16,128]{1,0:T(8,128)S(1)} %get-tuple-element.69.tab.tabv, s32[16,128]{1,0:T(8,128)S(1)} %get-tuple-element.69.tab.tabv, f32[2,8,128,128]{3,2,1,0:T(8,128)} %get-tuple-element.71.new_ref, f32[2,16,8,128]{3,2,1,0:T(8,128)} %get-tuple-element.72.old_ref, f32[256,128]{1,0:T(8,128)} %get-tuple-element.73.pan_ref, ...), custom_call_target="tpu_custom_call" | custom-call | tf_op jit(solution)/shard_map/cond/branch_1_fun/update/pallas_call | solution.py:569
Async XLA Ops:
  2.4 44.6 %copy-start = (f32[2,128,16,128]{3,2,1,0:T(8,128)S(1)}, f32[2,128,16,128]{3,2,1,0:T(8,128)}, u32[]{:S(2)}) copy-start(f32[2,128,16,128]{3,2,1,0:T(8,128)} %get-tuple-element.70) | copy-start | bytes 6291460 | tf_op jit(solution)/shard_map/cond
  2.4 44.6 %copy-start.10 = (s32[128]{0:T(128)S(1)}, s32[128]{0:T(128)}, u32[]{:S(2)}) copy-start(s32[128]{0:T(128)} %get-tuple-element.75) | copy-start | bytes 1540 | tf_op jit(solution)/shard_map/cond

commit v2 on v1

--- a/solution.py
+++ b/solution.py
@@ -87,12 +87,41 @@
     return result.astype(jnp.float32).reshape(row_cycles, panel_width, col_cycles, panel_width)
 
 
+def centred(x):
+    return x - PF * jnp.floor(x * INV + 0.5)
+
+
+def scaled_digits(a):
+    a = centred(a)
+    b = centred(a * 256.0)
+    both = jnp.concatenate([b, a], axis=1)
+    high = jnp.floor(both * (1.0 / 128.0) + 0.5)
+    return jnp.concatenate([high, both - 128.0 * high], axis=0).astype(BF16)
+
+
+def plain_digits(x):
+    high = jnp.floor(x * (1.0 / 256.0) + 0.5)
+    return jnp.concatenate([high.astype(BF16), (x - 256.0 * high).astype(BF16)], axis=0)
+
+
+def product(left, right):
+    both = jnp.dot(left, right, preferred_element_type=F32)
+    rows = both.shape[0] // 2
+    return centred(both[:rows]) * 128.0 + both[rows:]
+
+
+def one_hot_columns(values, hot):
+    high = jnp.floor(values * (1.0 / 256.0))
+    low = values - 256.0 * high
+    return 256.0 * jnp.dot(high.astype(BF16), hot, preferred_element_type=F32) + jnp.dot(
+        low.astype(BF16), hot, preferred_element_type=F32
+    )
+
+
 R_T1, R_T2, R_T3, R_O1, R_O2, R_O3, R_TV, R_OK = 0, 2, 4, 6, 8, 10, 12, 14
 
 
-def table_kernel(rank_ref, pivots_ref, out_ref):
-    me = rank_ref[0]
-    my_z, my_y = me >> 3, me & 7
+def fill_tables(my_z, my_y, pivots_ref, out_ref):
     sub = lax.broadcasted_iota(I32, (128, 128), 0)
     lane = lax.broadcasted_iota(I32, (128, 128), 1)
     eye = sub == lane
@@ -170,21 +199,13 @@
     out_ref[R_OK:R_OK + 1, :] = jnp.broadcast_to(worst, (1, 128)).astype(I32)
 
 
-def make_tables(row_rank, pivot_rows):
-    return pl.pallas_call(
-        table_kernel,
-        name="tables",
-        out_shape=jax.ShapeDtypeStruct((16, 128), I32),
-        in_specs=[
-            pl.BlockSpec(memory_space=pltpu.SMEM),
-            pl.BlockSpec(memory_space=pltpu.VMEM),
-        ],
-        out_specs=pl.BlockSpec(memory_space=pltpu.VMEM),
-    )(row_rank.reshape(1), pivot_rows.reshape(1, 128))
+FAR = (4, 3, 5, 2, 6, 1, 7)
 
 
 def exchange_kernel(
-    tab, mat, new_out, old_out, pan_out, opan_out,
+    pivots_ref, order_ref, linv_ref, uinv_ref, mat_hbm,
+    new_out, old_out, opan_out, low_out, linv_out, uinv_out, tab_out, flag_out,
+    mat, tabv, tab, pan, mat_sem, tab_sem,
     n1s, n1r, n2s, n2r, o1s, o1r, o2s, o2r, o3s,
     n1_ss, n1_rs, n2_ss, n2_rs, n3_ss, n3_rs, o1_ss, o1_rs, o2_ss, o2_rs, o3_ss, o3_rs,
     p1_ss, p1_rs, p2_ss, p2_rs,
@@ -223,29 +244,28 @@
         for dev in (minor_peer(0, step)[1], minor_peer(1, step)[1], col_peer(step)):
             pl.semaphore_signal(barrier, inc=1, device_id=dev, device_id_type=MESH)
 
+    fetch = pltpu.make_async_copy(mat_hbm, mat, mat_sem)
+    fetch.start()
+    fill_tables(z, y, pivots_ref, tabv)
+    to_scalar = pltpu.make_async_copy(tabv, tab, tab_sem)
+    to_scalar.start()
+    to_scalar.wait()
+    fetch.wait()
+
+    def entry(table, k, top):
+        return jnp.clip(tab[table, k], 0, top)
+
     def mat_tile(row, c):
         return mat[row * 2 + c]
 
     for c in range(2):
         for k in range(16):
-            n1s[c, k] = mat_tile(tab[R_T1 + c, k], c)
-
-    @pl.when(col == 0)
-    def _():
-        pan_out[...] = mat.reshape(4096, 128)[pl.ds(0, 256, stride=16), :]
-
-    @pl.when(rank == 0)
-    def _():
-        for c in range(2):
-            def body(u, carry):
-                o1s[c, u] = mat_tile(tab[R_O1 + c, u], c)
-                return carry
-            lax.fori_loop(0, 128, body, 0)
+            n1s[c, k] = mat_tile(entry(R_T1 + c, k, 255), c)
 
     pl.semaphore_wait(barrier, 21)
 
     n1 = []
-    for step in range(1, 8):
+    for step in FAR:
         for c in range(2):
             other, dev = minor_peer(c, step)
             minor = coords[c][1]
@@ -254,17 +274,8 @@
             d.start()
             n1.append(d)
 
-    p1 = []
-    for step in range(1, 8):
-        p1.append(copy(pan_out, pan_out, p1_ss.at[step], p1_rs, (rank, step)))
-
-    @pl.when(col == 0)
-    def _():
-        for d in p1:
-            d.start()
-
     o1 = []
-    for step in (1, 7, 2, 6, 3, 5, 4):
+    for step in FAR:
         for c in range(2):
             dev = (step if c == 0 else step * 8, col)
             o1.append(copy(o1s.at[c, pl.ds(16 * step, 16)], o1r.at[c],
@@ -272,15 +283,46 @@
 
     @pl.when(rank == 0)
     def _():
-        for d in o1:
-            d.start()
+        for n, step in enumerate((*FAR, 0)):
+            def body(k, carry):
+                for c in range(2):
+                    o1s[c, 16 * step + k] = mat_tile(entry(R_O1 + c, 16 * step + k, 127), c)
+                return carry
+            lax.fori_loop(0, 16, body, 0, unroll=4)
+            if step:
+                o1[2 * n].start()
+                o1[2 * n + 1].start()
         for c in range(2):
             o1r[c] = o1s[c, pl.ds(0, 16)]
 
+    p1 = []
+    for step in range(1, 8):
+        p1.append(copy(pan, pan, p1_ss.at[step], p1_rs, (rank, step)))
+
+    @pl.when(col == 0)
+    def _():
+        pan[...] = mat.reshape(4096, 128)[pl.ds(0, 256, stride=16), :]
+        for d in p1:
+            d.start()
+
     for c in range(2):
         minor = coords[c][1]
         n1r[c, pl.ds(2 * minor, 2)] = n1s[c, pl.ds(2 * minor, 2)]
 
+    sub = lax.broadcasted_iota(I32, (128, 128), 0)
+    order_hot = (sub == order_ref[...]).astype(BF16)
+    uinv = uinv_ref[...].astype(F32)
+    u_high = jnp.floor(uinv * (1.0 / 256.0))
+    u_low = uinv - 256.0 * u_high
+    uperm = 256.0 * jnp.dot(order_hot, u_high.astype(BF16), preferred_element_type=F32) + jnp.dot(
+        order_hot, u_low.astype(BF16), preferred_element_type=F32
+    )
+    uinv_out[...] = plain_digits(centred(uperm))
+    linv = linv_ref[...].astype(F32)
+    for c in range(2):
+        hot = (sub == tabv[R_O1 + c:R_O1 + c + 1, :]).astype(BF16)
+        linv_out[c] = scaled_digits(one_hot_columns(linv, hot))
+
     for d in n1:
         d.wait_recv()
 
@@ -288,10 +330,10 @@
     for c in range(2):
         plane = coords[c][0]
         for j in range(4):
-            row = n1r[c, tab[R_T2 + c, j]]
+            row = n1r[c, entry(R_T2 + c, j, 15)]
             n2s[c, j] = row
             n2r[c, plane * 4 + j] = row
-    for step in range(1, 8):
+    for step in FAR:
         for c in range(2):
             plane = coords[c][0]
             other, dev = plane_peer(c, step)
@@ -303,7 +345,7 @@
     o2 = [[], []]
     for c in range(2):
         plane, minor = coords[c]
-        for step in (1, 7, 2, 6, 3, 5, 4):
+        for step in FAR:
             dev = (row_of(c, step, minor), col)
             o2[c].append(copy(o2s.at[c, pl.ds(4 * step, 4)], o2r.at[c],
                               o2_ss.at[c, step], o2_rs.at[c], dev))
@@ -320,7 +362,7 @@
             @pl.when(plane == 0)
             def _():
                 def body(v, carry):
-                    o2s[c, v] = o1r[c, tab[R_O2 + c, v]]
+                    o2s[c, v] = o1r[c, entry(R_O2 + c, v, 15)]
                     return carry
                 lax.fori_loop(0, 32, body, 0)
                 for d in o2[c]:
@@ -333,7 +375,7 @@
     for c in range(2):
         minor = coords[c][1]
         for k in range(16):
-            row = n2r[c, tab[R_T3 + c, k]]
+            row = n2r[c, entry(R_T3 + c, k, 31)]
             new2d[pl.ds(c * 1024 + minor * 16 + k, 8, stride=128), :] = row
 
     sends = []
@@ -362,6 +404,12 @@
     for d in hops[1]:
         d.start()
     do_o2()
+
+    @pl.when(col != 0)
+    def _():
+        p1[0].wait_recv()
+
+    low_out[...] = centred(product(scaled_digits(pan[...]), uinv_out[...]))
     for h in range(2, 5):
         before = dict(zip(key(h - 1), hops[h - 1]))
         now = dict(zip(key(h), hops[h]))
@@ -379,9 +427,9 @@
             for c in range(2):
                 minor = coords[c][1]
                 for k in range(16):
-                    o3s[c, k] = o2r[c, tab[R_O3 + c, k]]
+                    o3s[c, k] = o2r[c, entry(R_O3 + c, k, 3)]
                 old_out[c, pl.ds(2 * minor, 2)] = o3s[c, pl.ds(2 * minor, 2)]
-                for step in range(1, 8):
+                for step in FAR:
                     other, dev = minor_peer(c, step)
                     d = copy(o3s.at[c, pl.ds(2 * other, 2)], old_out.at[c, pl.ds(2 * minor, 2)],
                              o3_ss.at[c, step], o3_rs.at[c, step], dev)
@@ -405,8 +453,12 @@
 
     @pl.when(col != 0)
     def _():
-        p1[0].wait_recv()
         p2[0].wait_recv()
+
+    for c in range(2):
+        for k in range(16):
+            tab_out[c, k] = tab[R_TV + c, k]
+    flag_out[0] = tab[R_OK, 0]
 
     for d in n1 + n2 + o3 + [d for h in hops for d in hops[h]]:
         d.wait_send()
@@ -428,8 +480,9 @@
             d.wait_send()
 
 
-def exchange(tables, mat):
+def exchange(pivot_rows, column_order, linv, uinv, mat):
     vmem = pl.BlockSpec(memory_space=pltpu.VMEM)
+    smem = pl.BlockSpec(memory_space=pltpu.SMEM)
     dma = pltpu.SemaphoreType.DMA
     tile = lambda *lead: pltpu.VMEM((*lead, 8, 128), F32)
     return pl.pallas_call(
@@ -438,12 +491,18 @@
         out_shape=(
             jax.ShapeDtypeStruct((2, 8, 128, 128), F32),
             jax.ShapeDtypeStruct((2, 16, 8, 128), F32),
+            jax.ShapeDtypeStruct((16, 128), F32),
             jax.ShapeDtypeStruct((256, 128), F32),
-            jax.ShapeDtypeStruct((16, 128), F32),
+            jax.ShapeDtypeStruct((2, 256, 256), BF16),
+            jax.ShapeDtypeStruct((256, 128), BF16),
+            jax.ShapeDtypeStruct((2, 16), I32),
+            jax.ShapeDtypeStruct((1,), I32),
         ),
-        in_specs=[pl.BlockSpec(memory_space=pltpu.SMEM), vmem],
-        out_specs=(vmem,) * 4,
+        in_specs=[vmem] * 4 + [pl.BlockSpec(memory_space=pl.ANY)],
+        out_specs=(vmem,) * 6 + (smem, smem),
         scratch_shapes=[
+            tile(512), pltpu.VMEM((16, 128), I32), pltpu.SMEM((16, 128), I32),
+            pltpu.VMEM((256, 128), F32), dma, dma,
             tile(2, 16), tile(2, 16), tile(2, 4), tile(2, 32), tile(2, 128), tile(2, 16),
             tile(2, 32), tile(2, 4), tile(2, 16),
             dma((2, 8)), dma((2, 8)), dma((2, 8)), dma((2, 8)),
@@ -451,94 +510,36 @@
             dma((2, 8)), dma((2,)), dma((2, 8)), dma((2,)), dma((2, 8)), dma((2, 8)),
             dma((8,)), dma, dma((8,)), dma,
         ],
-        compiler_params=pltpu.CompilerParams(collective_id=0, has_side_effects=True),
-    )(tables, mat)
-
-
-def centred(x):
-    return x - PF * jnp.floor(x * INV + 0.5)
-
-
-def scaled_digits(a):
-    a = centred(a)
-    b = centred(a * 256.0)
-    both = jnp.concatenate([b, a], axis=1)
-    high = jnp.floor(both * (1.0 / 128.0) + 0.5)
-    return jnp.concatenate([high, both - 128.0 * high], axis=0).astype(BF16)
-
-
-def plain_digits(x):
-    high = jnp.floor(x * (1.0 / 256.0) + 0.5)
-    return jnp.concatenate([high.astype(BF16), (x - 256.0 * high).astype(BF16)], axis=0)
-
-
-def product(left, right):
-    both = jnp.dot(left, right, preferred_element_type=F32)
-    rows = both.shape[0] // 2
-    return centred(both[:rows]) * 128.0 + both[rows:]
-
-
-def one_hot_columns(values, hot):
-    high = jnp.floor(values * (1.0 / 256.0))
-    low = values - 256.0 * high
-    return 256.0 * jnp.dot(high.astype(BF16), hot, preferred_element_type=F32) + jnp.dot(
-        low.astype(BF16), hot, preferred_element_type=F32
-    )
-
-
-def compute_kernel(
-    tab, tabv, new_ref, old_ref, pan_ref, opan_ref, order_ref, linv_ref, uinv_ref, mat_hbm,
-    out_ref, mat, pan, low, linv_d, low_d, sem,
+        compiler_params=pltpu.CompilerParams(
+            collective_id=0, has_side_effects=True, vmem_limit_bytes=24 << 20
+        ),
+    )(pivot_rows.reshape(1, 128), column_order.reshape(1, 128), linv, uinv, mat)
+
+
+def update_kernel(
+    tab, new_ref, old_ref, opan_ref, low_ref, linv_d, uinv_d, order_ref, mat_hbm,
+    out_hbm, mat, low, low_d, up_d, out, sem, out_sem,
 ):
     rank, col = lax.axis_index("row"), lax.axis_index("col")
     fetch = pltpu.make_async_copy(mat_hbm, mat, sem)
     fetch.start()
     sub = lax.broadcasted_iota(I32, (128, 128), 0)
     eye = sub == lax.broadcasted_iota(I32, (128, 128), 1)
-
-    pan[...] = pan_ref[...]
-
-    def patch_panel(k, carry):
-        slot = tab[R_TV, k]
+    mat2d = mat.reshape(4096, 128)
+    out2d = out.reshape(4096, 128)
+
+    low[...] = low_ref[...]
+    old_low = centred(product(scaled_digits(opan_ref[...]), uinv_d[...]))
+    for k in range(16):
+        slot = tab[0, k]
 
         @pl.when(slot >= 0)
         def _():
-            pan[pl.ds(slot, 1), :] = opan_ref[pl.ds(k, 1), :]
-        return carry
-    lax.fori_loop(0, 16, patch_panel, 0)
-
-    order_hot = (sub == order_ref[...]).astype(BF16)
-    uinv = uinv_ref[...].astype(F32)
-    u_high = jnp.floor(uinv * (1.0 / 256.0))
-    u_low = uinv - 256.0 * u_high
-    uperm = 256.0 * jnp.dot(order_hot, u_high.astype(BF16), preferred_element_type=F32) + jnp.dot(
-        order_hot, u_low.astype(BF16), preferred_element_type=F32
-    )
-    lower = centred(product(scaled_digits(pan[...]), plain_digits(centred(uperm))))
-    low[...] = jnp.where(lower < 0.0, lower + PF, lower)
+            low[pl.ds(slot, 1), :] = old_low[k:k + 1, :]
+    lower = low[...]
     top = jnp.where(rank == 0, jnp.where(eye, -1.0, 0.0), lower[:128])
-    low_d[...] = scaled_digits(jnp.concatenate([top, lower[128:]], axis=0))
-
-    linv = linv_ref[...].astype(F32)
-    for c in range(2):
-        hot = (sub == tabv[R_O1 + c:R_O1 + c + 1, :]).astype(BF16)
-        linv_d[c] = scaled_digits(one_hot_columns(linv, hot))
-
-    fetch.wait()
-
-    def patch_rows(k, carry):
-        for c in range(2):
-            slot = tab[R_TV + c, k]
-
-            @pl.when(slot >= 0)
-            def _():
-                mat[pl.ds(pl.multiple_of(slot * 16 + 8 * c, 8), 8), :] = old_ref[c, k]
-        return carry
-    lax.fori_loop(0, 16, patch_rows, 0)
-
-    @pl.when(rank == 0)
-    def _():
-        mat[0:2048, :] = jnp.zeros((2048, 128), F32)
+    low_d[0] = scaled_digits(top)
+    low_d[1] = scaled_digits(lower[128:])
 
     first_upper = None
     for pair in range(8):
@@ -547,55 +548,84 @@
         upper = centred(product(linv_d[c], plain_digits(x)))
         if pair == 0:
             first_upper = upper[:, :128]
-        update = product(low_d[...], plain_digits(upper))
-        for side in range(2):
-            rows = pl.ds(2 * pair + side, 256, stride=16)
-            value = mat[rows, :] - update[:, 128 * side:128 * side + 128]
-            out_ref[rows, :] = value - PF * jnp.floor((value + 0.5) * INV)
-
-    @pl.when(col == 0)
-    def _():
-        out_ref[pl.ds(0, 256, stride=16), :] = low[...]
-
-        @pl.when(rank == 0)
-        def _():
-            upper = jnp.where(first_upper < 0.0, first_upper + PF, first_upper)
-            out_ref[pl.ds(0, 128, stride=16), :] = one_hot_columns(upper, order_hot)
-
-
-def compute(tables, new, old, panel, old_panel, column_order, linv, uinv, mat):
+        up_d[pair] = plain_digits(upper)
+
+    fetch.wait()
+    for k in range(16):
+        for c in range(2):
+            slot = tab[c, k]
+
+            @pl.when(slot >= 0)
+            def _():
+                mat[slot, c] = old_ref[c, k]
+
+    @pl.when(rank == 0)
+    def _():
+        mat[0:128] = jnp.zeros((128, 2, 8, 128), F32)
+
+    sent = []
+    for half in range(2):
+        for pair in range(8):
+            c = pair // 4
+            change = product(low_d[half], up_d[pair])
+            for side in range(2):
+                rows = pl.ds(2048 * half + 2 * pair + side, 128, stride=16)
+                value = mat2d[rows, :] - change[:, 128 * side:128 * side + 128]
+                out2d[rows, :] = value - PF * jnp.floor((value + 0.5) * INV)
+            if pair == 0:
+                @pl.when(col == 0)
+                def _():
+                    part = low[128 * half:128 * half + 128, :]
+                    out2d[pl.ds(2048 * half, 128, stride=16), :] = jnp.where(
+                        part < 0.0, part + PF, part
+                    )
+
+                if half == 0:
+                    @pl.when((col == 0) & (rank == 0))
+                    def _():
+                        order_hot = (sub == order_ref[...]).astype(BF16)
+                        upper = jnp.where(first_upper < 0.0, first_upper + PF, first_upper)
+                        out2d[pl.ds(0, 128, stride=16), :] = one_hot_columns(upper, order_hot)
+            if pair % 4 == 3:
+                where = (pl.ds(128 * half, 128), c)
+                d = pltpu.make_async_copy(out.at[where], out_hbm.at[where], out_sem.at[half, c])
+                d.start()
+                sent.append(d)
+    for d in sent:
+        d.wait()
+
+
+def update(tab, new, old, old_panel, low, linv_d, uinv_d, column_order, mat):
     vmem = pl.BlockSpec(memory_space=pltpu.VMEM)
-    smem = pl.BlockSpec(memory_space=pltpu.SMEM)
+    whole = pltpu.VMEM((256, 2, 8, 128), F32)
     return pl.pallas_call(
-        compute_kernel,
+        update_kernel,
         name="update",
-        out_shape=jax.ShapeDtypeStruct((4096, 128), F32),
-        in_specs=[smem] + [vmem] * 8 + [pl.BlockSpec(memory_space=pl.ANY)],
-        out_specs=vmem,
+        out_shape=jax.ShapeDtypeStruct((256, 2, 8, 128), F32),
+        in_specs=[pl.BlockSpec(memory_space=pltpu.SMEM)] + [vmem] * 7
+        + [pl.BlockSpec(memory_space=pl.ANY)],
+        out_specs=pl.BlockSpec(memory_space=pl.ANY),
         scratch_shapes=[
-            pltpu.VMEM((4096, 128), F32),
-            pltpu.VMEM((256, 128), F32),
+            whole,
             pltpu.VMEM((256, 128), F32),
             pltpu.VMEM((2, 256, 256), BF16),
-            pltpu.VMEM((512, 256), BF16),
+            pltpu.VMEM((8, 256, 256), BF16),
+            whole,
             pltpu.SemaphoreType.DMA,
+            pltpu.SemaphoreType.DMA((2, 2)),
         ],
-    )(tables, tables, new, old, panel, old_panel, column_order, linv, uinv, mat)
-
-
-def fast_path(tables, matrix, column_order, lower_inverse, upper_inverse):
-    mat = matrix.reshape(4096, 128)
-    new, old, panel, old_panel = exchange(tables, matrix.reshape(512, 8, 128))
-    out = compute(tables, new, old, panel, old_panel, column_order.reshape(1, 128),
-                  lower_inverse, upper_inverse, mat)
-    return out.reshape(matrix.shape)
+        compiler_params=pltpu.CompilerParams(vmem_limit_bytes=24 << 20),
+    )(tab, new, old, old_panel, low, linv_d, uinv_d, column_order.reshape(1, 128), mat)
 
 
 def on_device(matrix, pivot_rows, column_order, lower_inverse, upper_inverse):
-    tables = make_tables(lax.axis_index("row"), pivot_rows)
+    new, old, old_panel, low, linv_d, uinv_d, tab, flag = exchange(
+        pivot_rows, column_order, lower_inverse, upper_inverse, matrix.reshape(512, 8, 128)
+    )
     return lax.cond(
-        tables[R_OK, 0] > 0,
-        lambda: fast_path(tables, matrix, column_order, lower_inverse, upper_inverse),
+        flag[0] > 0,
+        lambda: update(tab, new, old, old_panel, low, linv_d, uinv_d, column_order,
+                       matrix.reshape(256, 2, 8, 128)).reshape(matrix.shape),
         lambda: general_path(matrix, pivot_rows, column_order, lower_inverse, upper_inverse),
     )
 

time: 54.7 us -> 49.1 us (0.90)
  the two profiles are of different devices: /device:TPU:5 before, /device:TPU:2 now
where the time goes in v2:
time: 49.1 us; the launch traced here: 48.9 us
  Pallas kernels  47.8 us (97%)
  between operations  0.86 us (2%)
    pallas_call x1, Pallas kernels, exchange(): pl.pallas_call(exchange_kernel, name='exchange', out_shape=(jax.ShapeDtyp...  41.6 us
    pallas_call x1, Pallas kernels, update(): pl.pallas_call(update_kernel, name='update', out_shape=jax.ShapeDtypeStru...  6.16 us

profile of v2, /device:TPU:2, one launch (start us, length us, event | category | flops | bytes accessed | tf_op | source)
XLA Modules:
  0.0 48.9 jit_solution(17745525833606724785)
XLA Ops:
  0.0 0.0 copy-start.11
  0.0 0.0 copy-start
  0.0 0.0 copy-start.10
  0.0 0.0 copy-start.9
  0.0 0.0 copy-start.12
  0.0 41.6 %exchange.1 = (f32[2,8,128,128]{3,2,1,0:T(8,128)}, f32[2,16,8,128]{3,2,1,0:T(8,128)}, f32[16,128]{1,0:T(8,128)S(1)}, f32[256,128]{1,0:T(8,128)}, bf16[2,256,256]...) custom-call(s32[1,128]{1,0:T(1,128)} %bitcast.50, s32[1,128]{1,0:T(1,128)} %bitcast.48, ...), custom_call_target="tpu_custom_call" | custom-call | tf_op jit(solution)/shard_map/exchange/pallas_call | solution.py:488
  42.3 0.0 copy-done.11
  42.3 0.0 copy-done
  42.3 0.0 copy-done.10
  42.3 0.0 copy-done.9
  42.3 0.0 copy-done.12
  42.3 6.4 %conditional.1 = (f32[2,128,16,128]{3,2,1,0:T(8,128)}) conditional(s32[]{:T(128)} %bitcast.8, (f32[2,128,16,128]{3,2,1,0:T(8,128)S(1)}, s32[128]{0:T(128)S(1)}, s32[128]{0:T(128)S(1)}, s32[128,128]{1,0:T(8,128)S(1)}, s32[128,128]{1,0:T(8,128)S(1)}) %tuple.59, (s32[128]{0:T(128)S(1)}, f32[2,128,16,128]{3,2,1,0:T(8,128)S(1)}, s32[2,16]{1,0:T(2,128)}, ...), branch_computations={%region_0.3_spmd, %region_3.4_spmd} | conditional | flops 2036082944 | bytes 212554112 | solution.py:625
  42.6 6.2 %update.1 = f32[256,2,8,128]{3,2,1,0:T(8,128)} custom-call(s32[2,16]{1,0:T(2,128)} %get-tuple-element.77.tab, f32[2,8,128,128]{3,2,1,0:T(8,128)} %get-tuple-element.78.new_ref, f32[2,16,8,128]{3,2,1,0:T(8,128)} %get-tuple-element.79.old_ref, f32[16,128]{1,0:T(8,128)S(1)} %get-tuple-element.80.opan_ref, f32[256,128]{1,0:T(8,128)} %get-tuple-element.81.low_ref, ...), custom_call_target="tpu_custom_call" | custom-call | tf_op jit(solution)/shard_map/cond/branch_1_fun/update/pallas_call | solution.py:601
Async XLA Ops:
  0.0 42.3 %copy-start.11 = (s32[128]{0:T(128)S(1)}, s32[128]{0:T(128)}, u32[]{:S(2)}) copy-start(s32[128]{0:T(128)} %param.15) | copy-start | bytes 1540
  0.0 42.3 %copy-start = (f32[2,128,16,128]{3,2,1,0:T(8,128)S(1)}, f32[2,128,16,128]{3,2,1,0:T(8,128)}, u32[]{:S(2)}) copy-start(f32[2,128,16,128]{3,2,1,0:T(8,128)} %param.13) | copy-start | bytes 6291460
  0.0 42.3 %copy-start.10 = (s32[128,128]{1,0:T(8,128)S(1)}, s32[128,128]{1,0:T(8,128)}, u32[]{:S(2)}) copy-start(s32[128,128]{1,0:T(8,128)} %uinv_ref.1) | copy-start | bytes 196612
  0.0 42.3 %copy-start.9 = (s32[128,128]{1,0:T(8,128)S(1)}, s32[128,128]{1,0:T(8,128)}, u32[]{:S(2)}) copy-start(s32[128,128]{1,0:T(8,128)} %linv_ref.1) | copy-start | bytes 196612
  0.0 42.3 %copy-start.12 = (s32[128]{0:T(128)S(1)}, s32[128]{0:T(128)}, u32[]{:S(2)}) copy-start(s32[128]{0:T(128)} %param.14) | copy-start | bytes 1540

commit v3 on v2

--- a/solution.py
+++ b/solution.py
@@ -5,8 +5,6 @@
 from jax.experimental.pallas import tpu as pltpu
 from jax.sharding import PartitionSpec as P
 
-prime_modulus = 32749
-limb_divisors = (1, 32, 1024)
 PF = 32749.0
 INV = 1.0 / 32749.0
 MESH = pl.DeviceIdType.MESH
@@ -22,35 +20,6 @@
         array = array + lax.ppermute(array, axis, [(i, i ^ step) for i in range(count)])
         step *= 2
     return array
-
-
-def split_limbs(values):
-    return [(values // divisor % 32).astype(jnp.bfloat16) for divisor in limb_divisors]
-
-
-def modular_product(left_side, right_side):
-    left_limbs = split_limbs(left_side.astype(jnp.int32))
-    right_limbs = split_limbs(right_side.astype(jnp.int32))
-    outcome = jnp.zeros((left_side.shape[0], right_side.shape[1]), jnp.int32)
-    factor = 1
-    for degree in range(5):
-        limb_pairs = [
-            (left_degree, degree - left_degree)
-            for left_degree in range(3)
-            if 0 <= degree - left_degree < 3
-        ]
-        stacked_left = jnp.concatenate(
-            [left_limbs[limb_pair[0]] for limb_pair in limb_pairs], axis=1
-        )
-        stacked_right = jnp.concatenate(
-            [right_limbs[limb_pair[1]] for limb_pair in limb_pairs], axis=0
-        )
-        partial_sum = jnp.dot(
-            stacked_left, stacked_right, preferred_element_type=jnp.float32
-        ).astype(jnp.int32)
-        outcome = (outcome + partial_sum % prime_modulus * factor % prime_modulus) % prime_modulus
-        factor = factor * 32 % prime_modulus
-    return outcome
 
 
 def general_path(matrix, pivot_rows, column_order, lower_inverse, upper_inverse):
@@ -70,21 +39,21 @@
     picked = jnp.where(owned[:, None], flat[jnp.where(owned, local_slot, 0)], 0.0)
     top_rows = jnp.where(row_rank == 0, flat[:panel_width], 0.0)
     new_top, old_top = sum_over(picked, "row"), sum_over(top_rows, "row")
-    upper_all = modular_product(lower_inverse, new_top)
+    upper_all = modular_product(lower_inverse.astype(F32), new_top)
     targets = jnp.where(owned, local_slot, local_rows)
     swapped = flat.at[targets].set(old_top, mode="drop")
     panel = swapped[:, :panel_width][:, column_order]
     panel_all = sum_over(jnp.where(col_rank == 0, panel, 0.0), "col")
-    lower_all = modular_product(panel_all, upper_inverse)
+    lower_all = modular_product(panel_all, upper_inverse.astype(F32))
     permuted = upper_all.at[:, :panel_width].set(upper_all[:, column_order])
     upper_use = jnp.where(col_rank == 0, permuted, upper_all)
-    update = modular_product(lower_all, upper_use)
-    result = (swapped.astype(jnp.int32) - update) % prime_modulus
+    result = swapped - modular_product(lower_all, upper_use)
+    result = jnp.where(result < 0.0, result + PF, result)
     result = result.at[:, :panel_width].set(
         jnp.where(col_rank == 0, lower_all, result[:, :panel_width])
     )
     result = result.at[:panel_width].set(jnp.where(row_rank == 0, upper_use, result[:panel_width]))
-    return result.astype(jnp.float32).reshape(row_cycles, panel_width, col_cycles, panel_width)
+    return result.reshape(row_cycles, panel_width, col_cycles, panel_width)
 
 
 def centred(x):
@@ -108,6 +77,11 @@
     both = jnp.dot(left, right, preferred_element_type=F32)
     rows = both.shape[0] // 2
     return centred(both[:rows]) * 128.0 + both[rows:]
+
+
+def modular_product(left, right):
+    rest = centred(product(scaled_digits(left), plain_digits(right)))
+    return jnp.where(rest < 0.0, rest + PF, rest)
 
 
 def one_hot_columns(values, hot):
@@ -350,24 +324,23 @@
             o2[c].append(copy(o2s.at[c, pl.ds(4 * step, 4)], o2r.at[c],
                               o2_ss.at[c, step], o2_rs.at[c], dev))
 
-    def do_o2():
-        for c in range(2):
-            plane, minor = coords[c]
-
-            @pl.when((plane == 0) & (minor != 0))
-            def _():
-                copy(o1s.at[c, pl.ds(0, 16)], o1r.at[c], o1_ss.at[c, 0], o1_rs.at[c],
-                     (0, col)).wait_recv()
-
-            @pl.when(plane == 0)
-            def _():
-                def body(v, carry):
-                    o2s[c, v] = o1r[c, entry(R_O2 + c, v, 15)]
-                    return carry
-                lax.fori_loop(0, 32, body, 0)
-                for d in o2[c]:
-                    d.start()
-                o2r[c] = o2s[c, pl.ds(0, 4)]
+    for c in range(2):
+        plane, minor = coords[c]
+
+        @pl.when((plane == 0) & (minor != 0))
+        def _():
+            copy(o1s.at[c, pl.ds(0, 16)], o1r.at[c], o1_ss.at[c, 0], o1_rs.at[c],
+                 (0, col)).wait_recv()
+
+        @pl.when(plane == 0)
+        def _():
+            def body(v, carry):
+                o2s[c, v] = o1r[c, entry(R_O2 + c, v, 15)]
+                return carry
+            lax.fori_loop(0, 32, body, 0)
+            for d in o2[c]:
+                d.start()
+            o2r[c] = o2s[c, pl.ds(0, 4)]
 
     for d in n2:
         d.wait_recv()
@@ -378,63 +351,63 @@
             row = n2r[c, entry(R_T3 + c, k, 31)]
             new2d[pl.ds(c * 1024 + minor * 16 + k, 8, stride=128), :] = row
 
-    sends = []
-
-    def hop_copies(h):
-        found = []
-        for q in range(2):
-            for c in range(2):
-                minor = coords[c][1]
-                for way in range(2):
-                    if h == 4 and q != way:
-                        continue
-                    sign = 1 if way == 0 else -1
-                    block = (minor - sign * (h - 1)) % 8
-                    part = new_out.at[c, pl.ds(4 * q, 4), pl.ds(pl.multiple_of(16 * block, 16), 16), :]
-                    found.append(copy(part, part, n3_ss.at[c, h, way, q], n3_rs.at[c, h, way, q],
-                                      minor_peer(c, sign)[1]))
-        return found
-
-    hops = {h: hop_copies(h) for h in range(1, 5)}
-
-    def key(h):
-        return [(q, c, way) for q in range(2) for c in range(2) for way in range(2)
-                if not (h == 4 and q != way)]
-
-    for d in hops[1]:
-        d.start()
-    do_o2()
+    def part(c, block, e, count):
+        rows = pl.ds(pl.multiple_of(16 * block, 16), 16)
+        return new_out.at[c, pl.ds(e, count), rows, :]
+
+    def n3_copy(c, kind, way, q, block, e, count, offset):
+        piece = part(c, block % 8, e, count)
+        return copy(piece, piece, n3_ss.at[c, kind, way, q], n3_rs.at[c, kind, way, q],
+                    minor_peer(c, offset)[1])
+
+    both = [(c, way) for c in range(2) for way in range(2)]
+    two, one, three, four = {}, {}, {}, {}
+    for c, way in both:
+        minor = coords[c][1]
+        sign = 1 - 2 * way
+        one[c, way] = n3_copy(c, 1, way, 0, minor, 0, 8, sign)
+        for n in range(2):
+            q = n if way == 0 else 1 - n
+            two[c, way, n] = n3_copy(c, 0, way, n, minor, 4 * q, 4, 2 * sign)
+            three[c, way, n] = n3_copy(c, 2, way, n, minor - 2 * sign, 4 * q, 4, sign)
+        four[c, way] = n3_copy(c, 3, way, 0, minor - 2 * sign, 4 * way, 4, 2 * sign)
+    for n in range(2):
+        for c, way in both:
+            two[c, way, n].start()
+    for c, way in both:
+        one[c, way].start()
+
+    for c in range(2):
+        @pl.when(coords[c][0] != 0)
+        def _():
+            o2[c][0].wait_recv()
+
+    o3 = []
+    for c in range(2):
+        minor = coords[c][1]
+        for k in range(16):
+            o3s[c, k] = o2r[c, entry(R_O3 + c, k, 3)]
+        old_out[c, pl.ds(2 * minor, 2)] = o3s[c, pl.ds(2 * minor, 2)]
+        for step in FAR:
+            other, dev = minor_peer(c, step)
+            d = copy(o3s.at[c, pl.ds(2 * other, 2)], old_out.at[c, pl.ds(2 * minor, 2)],
+                     o3_ss.at[c, step], o3_rs.at[c, step], dev)
+            d.start()
+            o3.append(d)
 
     @pl.when(col != 0)
     def _():
         p1[0].wait_recv()
 
     low_out[...] = centred(product(scaled_digits(pan[...]), uinv_out[...]))
-    for h in range(2, 5):
-        before = dict(zip(key(h - 1), hops[h - 1]))
-        now = dict(zip(key(h), hops[h]))
-        for k in key(h - 1):
-            before[k].wait_recv()
-            if k in now:
-                now[k].start()
-        if h == 2:
-            o3 = []
-            for c in range(2):
-                @pl.when(coords[c][0] != 0)
-                def _():
-                    o2[c][0].wait_recv()
-
-            for c in range(2):
-                minor = coords[c][1]
-                for k in range(16):
-                    o3s[c, k] = o2r[c, entry(R_O3 + c, k, 3)]
-                old_out[c, pl.ds(2 * minor, 2)] = o3s[c, pl.ds(2 * minor, 2)]
-                for step in FAR:
-                    other, dev = minor_peer(c, step)
-                    d = copy(o3s.at[c, pl.ds(2 * other, 2)], old_out.at[c, pl.ds(2 * minor, 2)],
-                             o3_ss.at[c, step], o3_rs.at[c, step], dev)
-                    d.start()
-                    o3.append(d)
+
+    for n in range(2):
+        for c, way in both:
+            two[c, way, n].wait_recv()
+            if n == 0:
+                four[c, way].start()
+            three[c, way, n].start()
+
     for d in o3:
         d.wait_recv()
     p2 = []
@@ -448,7 +421,7 @@
         for d in p2:
             d.start()
 
-    for d in hops[4]:
+    for d in [*one.values(), *three.values(), *four.values()]:
         d.wait_recv()
 
     @pl.when(col != 0)
@@ -460,7 +433,7 @@
             tab_out[c, k] = tab[R_TV + c, k]
     flag_out[0] = tab[R_OK, 0]
 
-    for d in n1 + n2 + o3 + [d for h in hops for d in hops[h]]:
+    for d in [*n1, *n2, *o3, *one.values(), *two.values(), *three.values(), *four.values()]:
         d.wait_send()
 
     @pl.when(rank == 0)
@@ -489,12 +462,12 @@
         exchange_kernel,
         name="exchange",
         out_shape=(
-            jax.ShapeDtypeStruct((2, 8, 128, 128), F32),
-            jax.ShapeDtypeStruct((2, 16, 8, 128), F32),
-            jax.ShapeDtypeStruct((16, 128), F32),
-            jax.ShapeDtypeStruct((256, 128), F32),
-            jax.ShapeDtypeStruct((2, 256, 256), BF16),
-            jax.ShapeDtypeStruct((256, 128), BF16),
+            pltpu.VMEM((2, 8, 128, 128), F32),
+            pltpu.VMEM((2, 16, 8, 128), F32),
+            pltpu.VMEM((16, 128), F32),
+            pltpu.VMEM((256, 128), F32),
+            pltpu.VMEM((2, 256, 256), BF16),
+            pltpu.VMEM((256, 128), BF16),
             jax.ShapeDtypeStruct((2, 16), I32),
             jax.ShapeDtypeStruct((1,), I32),
         ),
@@ -506,7 +479,7 @@
             tile(2, 16), tile(2, 16), tile(2, 4), tile(2, 32), tile(2, 128), tile(2, 16),
             tile(2, 32), tile(2, 4), tile(2, 16),
             dma((2, 8)), dma((2, 8)), dma((2, 8)), dma((2, 8)),
-            dma((2, 5, 2, 2)), dma((2, 5, 2, 2)),
+            dma((2, 4, 2, 2)), dma((2, 4, 2, 2)),
             dma((2, 8)), dma((2,)), dma((2, 8)), dma((2,)), dma((2, 8)), dma((2, 8)),
             dma((8,)), dma, dma((8,)), dma,
         ],

time: 49.1 us -> 45.9 us (0.935)
  the two profiles are of different devices: /device:TPU:2 before, /device:TPU:5 now
where the time goes in v3:
time: 45.9 us; the launch traced here: 45.6 us
  Pallas kernels  44.5 us (97%)
  between operations  0.8 us (2%)
    pallas_call x1, Pallas kernels, exchange(): pl.pallas_call(exchange_kernel, name='exchange', out_shape=(pltpu.VMEM((2...  39.1 us
    pallas_call x1, Pallas kernels, update(): pl.pallas_call(update_kernel, name='update', out_shape=jax.ShapeDtypeStru...  5.47 us

profile of v3, /device:TPU:5, one launch (start us, length us, event | category | flops | bytes accessed | tf_op | source)
XLA Modules:
  0.0 45.6 jit_solution(7674567086119030266)
XLA Ops:
  0.0 0.0 copy-start.7
  0.0 0.0 copy-start.6
  0.0 0.0 copy-start.5
  0.0 0.0 copy-start.8
  0.0 39.1 %exchange.1 = (f32[2,8,128,128]{3,2,1,0:T(8,128)S(1)}, f32[2,16,8,128]{3,2,1,0:T(8,128)S(1)}, f32[16,128]{1,0:T(8,128)S(1)}, f32[256,128]{1,0:T(8,128)S(1)}, bf1...) custom-call(s32[1,128]{1,0:T(1,128)} %bitcast.37, ...), custom_call_target="tpu_custom_call" | custom-call | tf_op jit(solution)/shard_map/exchange/pallas_call | solution.py:461
  39.7 0.0 copy-done.7
  39.7 0.0 copy-done.6
  39.7 0.0 copy-done.5
  39.7 0.0 copy-done.8
  39.7 5.7 %conditional.1 = (f32[2,128,16,128]{3,2,1,0:T(8,128)}) conditional(s32[]{:T(128)} %bitcast.8, (f32[2,128,16,128]{3,2,1,0:T(8,128)}, s32[128]{0:T(128)S(1)}, s32[128]{0:T(128)S(1)}, s32[128,128]{1,0:T(8,128)S(1)}, s32[128,128]{1,0:T(8,128)S(1)}) %tuple.55, (s32[128]{0:T(128)S(1)}, f32[2,128,16,128]{3,2,1,0:T(8,128)}, s32[2,16]{1,0:T(2,128)}, ...), branch_computations={%region_0.3_spmd, %region_3.4_spmd} | conditional | flops 869542144 | bytes 174805280 | solution.py:598
  39.9 5.5 %update.1 = f32[256,2,8,128]{3,2,1,0:T(8,128)} custom-call(s32[2,16]{1,0:T(2,128)} %get-tuple-element.77.tab, f32[2,8,128,128]{3,2,1,0:T(8,128)S(1)} %get-tuple-element.78.new_ref, f32[2,16,8,128]{3,2,1,0:T(8,128)S(1)} %get-tuple-element.79.old_ref, f32[16,128]{1,0:T(8,128)S(1)} %get-tuple-element.80.opan_ref, f32[256,128]{1,0:T(8,128)S(1)} %get-tuple-element.81.low_ref, ...), custom_call_target="tpu_custom_call" | custom-call | tf_op jit(solution)/shard_map/cond/branch_1_fun/update/pallas_call | solution.py:574
Async XLA Ops:
  0.0 39.7 %copy-start.7 = (s32[128]{0:T(128)S(1)}, s32[128]{0:T(128)}, u32[]{:S(2)}) copy-start(s32[128]{0:T(128)} %param.15) | copy-start | bytes 1540
  0.0 39.7 %copy-start.6 = (s32[128,128]{1,0:T(8,128)S(1)}, s32[128,128]{1,0:T(8,128)}, u32[]{:S(2)}) copy-start(s32[128,128]{1,0:T(8,128)} %uinv_ref.1) | copy-start | bytes 196612
  0.0 39.7 %copy-start.5 = (s32[128,128]{1,0:T(8,128)S(1)}, s32[128,128]{1,0:T(8,128)}, u32[]{:S(2)}) copy-start(s32[128,128]{1,0:T(8,128)} %linv_ref.1) | copy-start | bytes 196612
  0.0 39.7 %copy-start.8 = (s32[128]{0:T(128)S(1)}, s32[128]{0:T(128)}, u32[]{:S(2)}) copy-start(s32[128]{0:T(128)} %param.14) | copy-start | bytes 1540

commit v4 on v3

--- a/solution.py
+++ b/solution.py
@@ -64,19 +64,20 @@
     a = centred(a)
     b = centred(a * 256.0)
     both = jnp.concatenate([b, a], axis=1)
-    high = jnp.floor(both * (1.0 / 128.0) + 0.5)
-    return jnp.concatenate([high, both - 128.0 * high], axis=0).astype(BF16)
+    high = 64.0 * jnp.floor(both * (1.0 / 64.0) + 0.5)
+    return jnp.concatenate([high, both - high], axis=0).astype(BF16)
 
 
 def plain_digits(x):
-    high = jnp.floor(x * (1.0 / 256.0) + 0.5)
+    high = jnp.floor(x * (1.0 / 256.0))
     return jnp.concatenate([high.astype(BF16), (x - 256.0 * high).astype(BF16)], axis=0)
 
 
 def product(left, right):
     both = jnp.dot(left, right, preferred_element_type=F32)
     rows = both.shape[0] // 2
-    return centred(both[:rows]) * 128.0 + both[rows:]
+    high = both[:rows]
+    return (high - (64.0 * PF) * jnp.floor(high * (INV / 64.0))) + both[rows:]
 
 
 def modular_product(left, right):
@@ -92,10 +93,10 @@
     )
 
 
-R_T1, R_T2, R_T3, R_O1, R_O2, R_O3, R_TV, R_OK = 0, 2, 4, 6, 8, 10, 12, 14
-
-
-def fill_tables(my_z, my_y, pivots_ref, out_ref):
+R_T2, R_T3, R_O1, R_O2, R_O3, R_OK = 2, 4, 6, 8, 10, 14
+
+
+def fill_tables(my_z, my_y, pivots_ref, first_ref, out_ref):
     sub = lax.broadcasted_iota(I32, (128, 128), 0)
     lane = lax.broadcasted_iota(I32, (128, 128), 1)
     eye = sub == lane
@@ -108,8 +109,13 @@
     owner = (pivots & 8191) >> 7
     slot_col = column(((pivots >> 13) << 7) | (pivots & 127))
     index_col = lax.broadcasted_iota(I32, (128, 1), 0).astype(F32)
-    good = jnp.ones((1, 128), jnp.bool_)
-    out_ref[...] = jnp.zeros_like(out_ref)
+    zero = jnp.zeros((1, 128), I32)
+    half, odd = t >> 1, t & 1
+
+    def first(start, residue):
+        return start + ((residue - start) & 7)
+
+    halves = []
     for c in range(2):
         if c == 0:
             key, plane, minor = owner, my_z, my_y
@@ -120,30 +126,42 @@
         full_col = key_col * 128.0 + index_col
         rank_col = jnp.sum(jnp.where(full_row < full_col, 1.0, 0.0), axis=1, keepdims=True)
 
-        def before(x):
+        def before(x, key_col=key_col):
             return jnp.sum(
                 jnp.where(key_col < x.astype(F32), 1.0, 0.0), axis=0, keepdims=True
             ).astype(I32)
 
-        def at_rank(values_col, s):
+        def at_rank(values_col, s, rank_col=rank_col):
             return jnp.sum(
                 jnp.where(rank_col == s.astype(F32), values_col, 0.0), axis=0, keepdims=True
             ).astype(I32)
 
-        def first(start, residue):
-            return start + ((residue - start) & 7)
-
-        zero = jnp.zeros((1, 128), I32)
-        half, odd = t >> 1, t & 1
         mine = zero + (plane * 8 + minor)
         start = before(mine)
         end = before(mine + 1)
         s = first(start, half) + 8 * odd
         slot = at_rank(slot_col, s)
         held = (s < end) & (t < 16)
-        out_ref[R_T1 + c:R_T1 + c + 1, :] = jnp.where(held, slot, 0)
-        out_ref[R_TV + c:R_TV + c + 1, :] = jnp.where(held, slot, -1)
-
+        slot = jnp.where(held, slot, -1)
+        first_ref[c:c + 1, :] = slot
+        if c == 0:
+            slot_first = column(slot)
+        else:
+            same = slot_first == slot.astype(F32)
+            place = jnp.sum(jnp.where(same, index_col, 0.0), axis=0, keepdims=True)
+            first_ref[2:3, :] = place.astype(I32)
+        halves.append((plane, minor, key_col, before, at_rank))
+
+    def rest():
+        good = jnp.ones((1, 128), jnp.bool_)
+        out_ref[...] = jnp.zeros_like(out_ref)
+        for c in range(2):
+            good = fill_rest(c, good)
+        worst = jnp.min(jnp.where(good, 1.0, 0.0), axis=1, keepdims=True)
+        out_ref[R_OK:R_OK + 1, :] = jnp.broadcast_to(worst, (1, 128)).astype(I32)
+
+    def fill_rest(c, good):
+        plane, minor, key_col, before, at_rank = halves[c]
         plane_start = before(zero + plane * 8)
         my_first = first(plane_start, minor)
         s = my_first + 8 * t
@@ -169,8 +187,9 @@
         if c == 0:
             good = good & (before(t + 1) - before(t) <= 16)
         good = good & (before(t * 8 + 8) - before(t * 8) <= 32)
-    worst = jnp.min(jnp.where(good, 1.0, 0.0), axis=1, keepdims=True)
-    out_ref[R_OK:R_OK + 1, :] = jnp.broadcast_to(worst, (1, 128)).astype(I32)
+        return good
+
+    return rest
 
 
 FAR = (4, 3, 5, 2, 6, 1, 7)
@@ -178,8 +197,8 @@
 
 def exchange_kernel(
     pivots_ref, order_ref, linv_ref, uinv_ref, mat_hbm,
-    new_out, old_out, opan_out, low_out, linv_out, uinv_out, tab_out, flag_out,
-    mat, tabv, tab, pan, mat_sem, tab_sem,
+    new_out, old_out, opan_out, low_out, low_d_out, linv_out, uinv_out, mat_out, tab_out, flag_out,
+    mat, firstv, first, tabv, tab, pan, mat_sem, first_sem, tab_sem,
     n1s, n1r, n2s, n2r, o1s, o1r, o2s, o2r, o3s,
     n1_ss, n1_rs, n2_ss, n2_rs, n3_ss, n3_rs, o1_ss, o1_rs, o2_ss, o2_rs, o3_ss, o3_rs,
     p1_ss, p1_rs, p2_ss, p2_rs,
@@ -220,8 +239,8 @@
 
     fetch = pltpu.make_async_copy(mat_hbm, mat, mat_sem)
     fetch.start()
-    fill_tables(z, y, pivots_ref, tabv)
-    to_scalar = pltpu.make_async_copy(tabv, tab, tab_sem)
+    fill_rest = fill_tables(z, y, pivots_ref, firstv, tabv)
+    to_scalar = pltpu.make_async_copy(firstv, first, first_sem)
     to_scalar.start()
     to_scalar.wait()
     fetch.wait()
@@ -234,7 +253,7 @@
 
     for c in range(2):
         for k in range(16):
-            n1s[c, k] = mat_tile(entry(R_T1 + c, k, 255), c)
+            n1s[c, k] = mat_tile(jnp.clip(first[c, k], 0, 255), c)
 
     pl.semaphore_wait(barrier, 21)
 
@@ -247,6 +266,11 @@
                      n1_ss.at[c, step], n1_rs.at[c, step], dev)
             d.start()
             n1.append(d)
+
+    fill_rest()
+    to_scalar = pltpu.make_async_copy(tabv, tab, tab_sem)
+    to_scalar.start()
+    to_scalar.wait()
 
     o1 = []
     for step in FAR:
@@ -283,7 +307,13 @@
         minor = coords[c][1]
         n1r[c, pl.ds(2 * minor, 2)] = n1s[c, pl.ds(2 * minor, 2)]
 
+    mat2d = mat.reshape(4096, 128)
+    for e in range(16):
+        upper_half = mat2d[pl.ds(e, 128, stride=16), :]
+        mat_out[e, 0:128, :] = jnp.where(rank == 0, 0.0, upper_half)
+        mat_out[e, 128:256, :] = mat2d[pl.ds(2048 + e, 128, stride=16), :]
     sub = lax.broadcasted_iota(I32, (128, 128), 0)
+    eye = sub == lax.broadcasted_iota(I32, (128, 128), 1)
     order_hot = (sub == order_ref[...]).astype(BF16)
     uinv = uinv_ref[...].astype(F32)
     u_high = jnp.floor(uinv * (1.0 / 256.0))
@@ -399,7 +429,11 @@
     def _():
         p1[0].wait_recv()
 
-    low_out[...] = centred(product(scaled_digits(pan[...]), uinv_out[...]))
+    lower = centred(product(scaled_digits(pan[...]), uinv_out[...]))
+    low_out[...] = lower
+    top = jnp.where(rank == 0, jnp.where(eye, -1.0, 0.0), lower[:128])
+    low_d_out[0] = scaled_digits(top)
+    low_d_out[1] = scaled_digits(lower[128:])
 
     for n in range(2):
         for c, way in both:
@@ -428,9 +462,9 @@
     def _():
         p2[0].wait_recv()
 
-    for c in range(2):
+    for c in range(3):
         for k in range(16):
-            tab_out[c, k] = tab[R_TV + c, k]
+            tab_out[c, k] = first[c, k]
     flag_out[0] = tab[R_OK, 0]
 
     for d in [*n1, *n2, *o3, *one.values(), *two.values(), *three.values(), *four.values()]:
@@ -465,17 +499,20 @@
             pltpu.VMEM((2, 8, 128, 128), F32),
             pltpu.VMEM((2, 16, 8, 128), F32),
             pltpu.VMEM((16, 128), F32),
-            pltpu.VMEM((256, 128), F32),
+            jax.ShapeDtypeStruct((256, 128), F32),
             pltpu.VMEM((2, 256, 256), BF16),
-            pltpu.VMEM((256, 128), BF16),
-            jax.ShapeDtypeStruct((2, 16), I32),
+            jax.ShapeDtypeStruct((2, 256, 256), BF16),
+            jax.ShapeDtypeStruct((256, 128), BF16),
+            pltpu.VMEM((16, 256, 128), F32),
+            jax.ShapeDtypeStruct((3, 16), I32),
             jax.ShapeDtypeStruct((1,), I32),
         ),
         in_specs=[vmem] * 4 + [pl.BlockSpec(memory_space=pl.ANY)],
-        out_specs=(vmem,) * 6 + (smem, smem),
+        out_specs=(vmem,) * 8 + (smem, smem),
         scratch_shapes=[
-            tile(512), pltpu.VMEM((16, 128), I32), pltpu.SMEM((16, 128), I32),
-            pltpu.VMEM((256, 128), F32), dma, dma,
+            tile(512), pltpu.VMEM((8, 128), I32), pltpu.SMEM((8, 128), I32),
+            pltpu.VMEM((16, 128), I32), pltpu.SMEM((16, 128), I32),
+            pltpu.VMEM((256, 128), F32), dma, dma, dma,
             tile(2, 16), tile(2, 16), tile(2, 4), tile(2, 32), tile(2, 128), tile(2, 16),
             tile(2, 32), tile(2, 4), tile(2, 16),
             dma((2, 8)), dma((2, 8)), dma((2, 8)), dma((2, 8)),
@@ -490,29 +527,19 @@
 
 
 def update_kernel(
-    tab, new_ref, old_ref, opan_ref, low_ref, linv_d, uinv_d, order_ref, mat_hbm,
-    out_hbm, mat, low, low_d, up_d, out, sem, out_sem,
+    tab, new_ref, old_ref, opan_ref, low_ref, low_d, linv_d, uinv_d, mat, order_ref,
+    out_hbm, up_d, out, late, opan, out_sem,
 ):
     rank, col = lax.axis_index("row"), lax.axis_index("col")
-    fetch = pltpu.make_async_copy(mat_hbm, mat, sem)
-    fetch.start()
-    sub = lax.broadcasted_iota(I32, (128, 128), 0)
-    eye = sub == lax.broadcasted_iota(I32, (128, 128), 1)
-    mat2d = mat.reshape(4096, 128)
-    out2d = out.reshape(4096, 128)
-
-    low[...] = low_ref[...]
-    old_low = centred(product(scaled_digits(opan_ref[...]), uinv_d[...]))
-    for k in range(16):
-        slot = tab[0, k]
-
-        @pl.when(slot >= 0)
-        def _():
-            low[pl.ds(slot, 1), :] = old_low[k:k + 1, :]
-    lower = low[...]
-    top = jnp.where(rank == 0, jnp.where(eye, -1.0, 0.0), lower[:128])
-    low_d[0] = scaled_digits(top)
-    low_d[1] = scaled_digits(lower[128:])
+    out2d = out.reshape(257 * 16, 128)
+    late2d = late.reshape(256, 128)
+    old2d = old_ref.reshape(256, 128)
+
+    def positive(x):
+        return jnp.where(x < 0.0, x + PF, x)
+
+    def reduced(x):
+        return x - PF * jnp.floor((x + 0.5) * INV)
 
     first_upper = None
     for pair in range(8):
@@ -523,18 +550,21 @@
             first_upper = upper[:, :128]
         up_d[pair] = plain_digits(upper)
 
-    fetch.wait()
+    opan[0:16, :] = opan_ref[...]
     for k in range(16):
-        for c in range(2):
-            slot = tab[c, k]
-
-            @pl.when(slot >= 0)
-            def _():
-                mat[slot, c] = old_ref[c, k]
-
-    @pl.when(rank == 0)
-    def _():
-        mat[0:128] = jnp.zeros((128, 2, 8, 128), F32)
+        opan[16 + k:17 + k, :] = opan_ref[pl.ds(jnp.clip(tab[2, k], 0, 15), 1), :]
+    old_low = centred(product(scaled_digits(opan[...]), uinv_d[...]))
+    old_d = [scaled_digits(old_low[:16]), scaled_digits(old_low[16:])]
+    for pair in range(8):
+        c = pair // 4
+        change = product(old_d[c], up_d[pair])
+        for side in range(2):
+            e = (2 * pair + side) % 8
+            value = old2d[pl.ds(128 * c + e, 16, stride=8), :]
+            value = reduced(value - change[:, 128 * side:128 * side + 128])
+            if pair == 0 and side == 0:
+                value = jnp.where(col == 0, positive(old_low[:16]), value)
+            late2d[pl.ds(128 * c + e, 16, stride=8), :] = value
 
     sent = []
     for half in range(2):
@@ -542,24 +572,29 @@
             c = pair // 4
             change = product(low_d[half], up_d[pair])
             for side in range(2):
-                rows = pl.ds(2048 * half + 2 * pair + side, 128, stride=16)
-                value = mat2d[rows, :] - change[:, 128 * side:128 * side + 128]
-                out2d[rows, :] = value - PF * jnp.floor((value + 0.5) * INV)
+                e = 2 * pair + side
+                value = mat[e, 128 * half:128 * half + 128, :]
+                out2d[pl.ds(2048 * half + e, 128, stride=16), :] = reduced(
+                    value - change[:, 128 * side:128 * side + 128]
+                )
             if pair == 0:
                 @pl.when(col == 0)
                 def _():
-                    part = low[128 * half:128 * half + 128, :]
-                    out2d[pl.ds(2048 * half, 128, stride=16), :] = jnp.where(
-                        part < 0.0, part + PF, part
-                    )
+                    part = low_ref[128 * half:128 * half + 128, :]
+                    out2d[pl.ds(2048 * half, 128, stride=16), :] = positive(part)
 
                 if half == 0:
                     @pl.when((col == 0) & (rank == 0))
                     def _():
+                        sub = lax.broadcasted_iota(I32, (128, 128), 0)
                         order_hot = (sub == order_ref[...]).astype(BF16)
-                        upper = jnp.where(first_upper < 0.0, first_upper + PF, first_upper)
-                        out2d[pl.ds(0, 128, stride=16), :] = one_hot_columns(upper, order_hot)
+                        out2d[pl.ds(0, 128, stride=16), :] = one_hot_columns(
+                            positive(first_upper), order_hot
+                        )
             if pair % 4 == 3:
+                for k in range(16):
+                    slot = tab[c, k]
+                    out[jnp.where((slot >> 7) == half, slot, 256), c] = late[c, k]
                 where = (pl.ds(128 * half, 128), c)
                 d = pltpu.make_async_copy(out.at[where], out_hbm.at[where], out_sem.at[half, c])
                 d.start()
@@ -568,37 +603,32 @@
         d.wait()
 
 
-def update(tab, new, old, old_panel, low, linv_d, uinv_d, column_order, mat):
+def update(tab, new, old, old_panel, low, low_d, linv_d, uinv_d, mat, column_order):
     vmem = pl.BlockSpec(memory_space=pltpu.VMEM)
-    whole = pltpu.VMEM((256, 2, 8, 128), F32)
     return pl.pallas_call(
         update_kernel,
         name="update",
         out_shape=jax.ShapeDtypeStruct((256, 2, 8, 128), F32),
-        in_specs=[pl.BlockSpec(memory_space=pltpu.SMEM)] + [vmem] * 7
-        + [pl.BlockSpec(memory_space=pl.ANY)],
+        in_specs=[pl.BlockSpec(memory_space=pltpu.SMEM)] + [vmem] * 9,
         out_specs=pl.BlockSpec(memory_space=pl.ANY),
         scratch_shapes=[
-            whole,
-            pltpu.VMEM((256, 128), F32),
-            pltpu.VMEM((2, 256, 256), BF16),
             pltpu.VMEM((8, 256, 256), BF16),
-            whole,
-            pltpu.SemaphoreType.DMA,
+            pltpu.VMEM((257, 2, 8, 128), F32),
+            pltpu.VMEM((2, 16, 8, 128), F32),
+            pltpu.VMEM((32, 128), F32),
             pltpu.SemaphoreType.DMA((2, 2)),
         ],
         compiler_params=pltpu.CompilerParams(vmem_limit_bytes=24 << 20),
-    )(tab, new, old, old_panel, low, linv_d, uinv_d, column_order.reshape(1, 128), mat)
+    )(tab, new, old, old_panel, low, low_d, linv_d, uinv_d, mat, column_order.reshape(1, 128))
 
 
 def on_device(matrix, pivot_rows, column_order, lower_inverse, upper_inverse):
-    new, old, old_panel, low, linv_d, uinv_d, tab, flag = exchange(
+    *parts, tab, flag = exchange(
         pivot_rows, column_order, lower_inverse, upper_inverse, matrix.reshape(512, 8, 128)
     )
     return lax.cond(
         flag[0] > 0,
-        lambda: update(tab, new, old, old_panel, low, linv_d, uinv_d, column_order,
-                       matrix.reshape(256, 2, 8, 128)).reshape(matrix.shape),
+        lambda: update(tab, *parts, column_order).reshape(matrix.shape),
         lambda: general_path(matrix, pivot_rows, column_order, lower_inverse, upper_inverse),
     )
 

time: 45.9 us -> 45.4 us (0.989)
    pallas_call x1, Pallas kernels: 5.47 us -> 4.58 us  [update(): pl.pallas_call(update_kernel, name='update', out_shape=jax.ShapeDtypeStru...]
where the time goes in v4:
time: 45.4 us; the launch traced here: 45.2 us
  Pallas kernels  44.1 us (97%)
  between operations  0.83 us (2%)
    pallas_call x1, Pallas kernels, exchange(): pl.pallas_call(exchange_kernel, name='exchange', out_shape=(pltpu.VMEM((2...  39.5 us
    pallas_call x1, Pallas kernels, update(): pl.pallas_call(update_kernel, name='update', out_shape=jax.ShapeDtypeStru...  4.58 us

profile of v4, /device:TPU:5, one launch (start us, length us, event | category | flops | bytes accessed | tf_op | source)
XLA Modules:
  0.0 45.2 jit_solution(3563310203786164041)
XLA Ops:
  0.0 0.0 copy-start.7
  0.0 39.5 %exchange.1 = (f32[2,8,128,128]{3,2,1,0:T(8,128)S(1)}, f32[2,16,8,128]{3,2,1,0:T(8,128)S(1)}, f32[16,128]{1,0:T(8,128)S(1)}, f32[256,128]{1,0:T(8,128)}, bf16[2,...) custom-call(s32[1,128]{1,0:T(1,128)} %bitcast.35, ...), custom_call_target="tpu_custom_call" | custom-call | tf_op jit(solution)/shard_map/exchange/pallas_call | solution.py:495
  40.2 0.0 copy-done.7
  40.2 4.8 %conditional.1 = (f32[2,128,16,128]{3,2,1,0:T(8,128)}) conditional(s32[]{:T(128)} %bitcast.7, (f32[2,128,16,128]{3,2,1,0:T(8,128)}, s32[128]{0:T(128)}, s32[128]{0:T(128)S(1)}, s32[128,128]{1,0:T(8,128)}, s32[128,128]{1,0:T(8,128)}) %tuple.51, (s32[128]{0:T(128)S(1)}, s32[3,16]{1,0:T(4,128)}, f32[2,8,128,128]{3,2,1,0:T(8,128)S(1)}, ...), branch_computations={%region_0.3_spmd, %region_3.4_spmd} | conditional | flops 867625216 | bytes 175202688 | solution.py:629
  40.4 4.6 %update.1 = f32[256,2,8,128]{3,2,1,0:T(8,128)} custom-call(s32[3,16]{1,0:T(4,128)} %get-tuple-element.79.tab, f32[2,8,128,128]{3,2,1,0:T(8,128)S(1)} %get-tuple-element.80.new_ref, f32[2,16,8,128]{3,2,1,0:T(8,128)S(1)} %get-tuple-element.81.old_ref, f32[16,128]{1,0:T(8,128)S(1)} %get-tuple-element.82.opan_ref, f32[256,128]{1,0:T(8,128)} %get-tuple-element.83.low_ref, ...), custom_call_target="tpu_custom_call" | custom-call | tf_op jit(solution)/shard_map/cond/branch_1_fun/update/pallas_call | solution.py:608
Async XLA Ops:
  0.0 40.2 %copy-start.7 = (s32[128]{0:T(128)S(1)}, s32[128]{0:T(128)}, u32[]{:S(2)}) copy-start(s32[128]{0:T(128)} %param.15) | copy-start | bytes 1540

commit v5 on v4

--- a/solution.py
+++ b/solution.py
@@ -196,12 +196,14 @@
 
 
 def exchange_kernel(
-    pivots_ref, order_ref, linv_ref, uinv_ref, mat_hbm,
+    pivots_hbm, order_hbm, linv_hbm, uinv_hbm, mat_hbm,
     new_out, old_out, opan_out, low_out, low_d_out, linv_out, uinv_out, mat_out, tab_out, flag_out,
+    pivots_ref, order_ref, linv_ref, uinv_ref, in_sem,
     mat, firstv, first, tabv, tab, pan, mat_sem, first_sem, tab_sem,
+    p1s, p1r, p2s, p2r, p3s,
     n1s, n1r, n2s, n2r, o1s, o1r, o2s, o2r, o3s,
     n1_ss, n1_rs, n2_ss, n2_rs, n3_ss, n3_rs, o1_ss, o1_rs, o2_ss, o2_rs, o3_ss, o3_rs,
-    p1_ss, p1_rs, p2_ss, p2_rs,
+    p1_ss, p1_rs,
 ):
     rank = lax.axis_index("row")
     col = lax.axis_index("col")
@@ -237,8 +239,19 @@
         for dev in (minor_peer(0, step)[1], minor_peer(1, step)[1], col_peer(step)):
             pl.semaphore_signal(barrier, inc=1, device_id=dev, device_id_type=MESH)
 
+    small = [
+        pltpu.make_async_copy(src, dst, in_sem.at[n])
+        for n, (src, dst) in enumerate((
+            (pivots_hbm, pivots_ref), (order_hbm, order_ref),
+            (linv_hbm, linv_ref), (uinv_hbm, uinv_ref),
+        ))
+    ]
+    small[0].start()
     fetch = pltpu.make_async_copy(mat_hbm, mat, mat_sem)
     fetch.start()
+    for d in small[1:]:
+        d.start()
+    small[0].wait()
     fill_rest = fill_tables(z, y, pivots_ref, firstv, tabv)
     to_scalar = pltpu.make_async_copy(firstv, first, first_sem)
     to_scalar.start()
@@ -303,6 +316,13 @@
         for d in p1:
             d.start()
 
+    p_one = [copy(p1s.at[pl.ds(16 * step, 16)], p1r, o1_ss.at[2, step], o1_rs.at[2], (step, col))
+             for step in FAR]
+    p_two = [copy(p2s.at[step], p2r.at[0], o2_ss.at[2, step], o2_rs.at[2],
+                  (row_of(0, step, y), col)) for step in FAR]
+    p_three = [copy(p3s.at[minor_peer(0, step)[0]], opan_out.at[y], o3_ss.at[2, step],
+                    o3_rs.at[2, step], minor_peer(0, step)[1]) for step in FAR]
+
     for c in range(2):
         minor = coords[c][1]
         n1r[c, pl.ds(2 * minor, 2)] = n1s[c, pl.ds(2 * minor, 2)]
@@ -312,6 +332,8 @@
         upper_half = mat2d[pl.ds(e, 128, stride=16), :]
         mat_out[e, 0:128, :] = jnp.where(rank == 0, 0.0, upper_half)
         mat_out[e, 128:256, :] = mat2d[pl.ds(2048 + e, 128, stride=16), :]
+    for d in small[1:]:
+        d.wait()
     sub = lax.broadcasted_iota(I32, (128, 128), 0)
     eye = sub == lax.broadcasted_iota(I32, (128, 128), 1)
     order_hot = (sub == order_ref[...]).astype(BF16)
@@ -346,6 +368,18 @@
             d.start()
             n2.append(d)
 
+    @pl.when(col != 0)
+    def _():
+        p1[0].wait_recv()
+
+    @pl.when(rank == 0)
+    def _():
+        for k in range(128):
+            p1s[k:k + 1, :] = pan[pl.ds(entry(R_O1, k, 127), 1), :]
+        for d in p_one:
+            d.start()
+        p1r[...] = p1s[0:16, :]
+
     o2 = [[], []]
     for c in range(2):
         plane, minor = coords[c]
@@ -371,6 +405,18 @@
             for d in o2[c]:
                 d.start()
             o2r[c] = o2s[c, pl.ds(0, 4)]
+
+    @pl.when((z == 0) & (y != 0))
+    def _():
+        p_one[0].wait_recv()
+
+    @pl.when(z == 0)
+    def _():
+        for v in range(32):
+            p2s[v // 4, v % 4:v % 4 + 1, :] = p1r[pl.ds(entry(R_O2, v, 15), 1), :]
+        for d in p_two:
+            d.start()
+        p2r[0] = p2s[0]
 
     for d in n2:
         d.wait_recv()
@@ -425,9 +471,15 @@
             d.start()
             o3.append(d)
 
-    @pl.when(col != 0)
-    def _():
-        p1[0].wait_recv()
+    @pl.when(z != 0)
+    def _():
+        p_two[0].wait_recv()
+
+    for k in range(16):
+        p3s[k // 2, k % 2:k % 2 + 1, :] = p2r[0, pl.ds(entry(R_O3, k, 3), 1), :]
+    for d in p_three:
+        d.start()
+    opan_out[y] = p3s[y]
 
     lower = centred(product(scaled_digits(pan[...]), uinv_out[...]))
     low_out[...] = lower
@@ -442,54 +494,40 @@
                 four[c, way].start()
             three[c, way, n].start()
 
-    for d in o3:
+    for d in o3 + p_three:
         d.wait_recv()
-    p2 = []
-    for step in range(1, 8):
-        p2.append(copy(opan_out, opan_out, p2_ss.at[step], p2_rs, (rank, step)))
-
-    @pl.when(col == 0)
-    def _():
-        for k in range(16):
-            opan_out[k:k + 1, :] = old_out[0, k, 0:1, :]
-        for d in p2:
-            d.start()
-
     for d in [*one.values(), *three.values(), *four.values()]:
         d.wait_recv()
-
-    @pl.when(col != 0)
-    def _():
-        p2[0].wait_recv()
 
     for c in range(3):
         for k in range(16):
             tab_out[c, k] = first[c, k]
     flag_out[0] = tab[R_OK, 0]
 
-    for d in [*n1, *n2, *o3, *one.values(), *two.values(), *three.values(), *four.values()]:
+    for d in [*n1, *n2, *o3, *p_three, *one.values(), *two.values(), *three.values(), *four.values()]:
         d.wait_send()
 
     @pl.when(rank == 0)
     def _():
-        for d in o1:
+        for d in o1 + p_one:
             d.wait_send()
 
     for c in range(2):
         @pl.when(coords[c][0] == 0)
         def _():
-            for d in o2[c]:
+            for d in o2[c] + (p_two if c == 0 else []):
                 d.wait_send()
 
     @pl.when(col == 0)
     def _():
-        for d in p1 + p2:
+        for d in p1:
             d.wait_send()
 
 
 def exchange(pivot_rows, column_order, linv, uinv, mat):
     vmem = pl.BlockSpec(memory_space=pltpu.VMEM)
     smem = pl.BlockSpec(memory_space=pltpu.SMEM)
+    hbm = pl.BlockSpec(memory_space=pl.ANY)
     dma = pltpu.SemaphoreType.DMA
     tile = lambda *lead: pltpu.VMEM((*lead, 8, 128), F32)
     return pl.pallas_call(
@@ -498,7 +536,7 @@
         out_shape=(
             pltpu.VMEM((2, 8, 128, 128), F32),
             pltpu.VMEM((2, 16, 8, 128), F32),
-            pltpu.VMEM((16, 128), F32),
+            jax.ShapeDtypeStruct((8, 8, 128), F32),
             jax.ShapeDtypeStruct((256, 128), F32),
             pltpu.VMEM((2, 256, 256), BF16),
             jax.ShapeDtypeStruct((2, 256, 256), BF16),
@@ -507,18 +545,21 @@
             jax.ShapeDtypeStruct((3, 16), I32),
             jax.ShapeDtypeStruct((1,), I32),
         ),
-        in_specs=[vmem] * 4 + [pl.BlockSpec(memory_space=pl.ANY)],
+        in_specs=[hbm] * 5,
         out_specs=(vmem,) * 8 + (smem, smem),
         scratch_shapes=[
+            pltpu.VMEM((1, 128), I32), pltpu.VMEM((1, 128), I32),
+            pltpu.VMEM((128, 128), I32), pltpu.VMEM((128, 128), I32), dma((4,)),
             tile(512), pltpu.VMEM((8, 128), I32), pltpu.SMEM((8, 128), I32),
             pltpu.VMEM((16, 128), I32), pltpu.SMEM((16, 128), I32),
             pltpu.VMEM((256, 128), F32), dma, dma, dma,
+            pltpu.VMEM((128, 128), F32), pltpu.VMEM((16, 128), F32), tile(8), tile(1), tile(8),
             tile(2, 16), tile(2, 16), tile(2, 4), tile(2, 32), tile(2, 128), tile(2, 16),
             tile(2, 32), tile(2, 4), tile(2, 16),
             dma((2, 8)), dma((2, 8)), dma((2, 8)), dma((2, 8)),
             dma((2, 4, 2, 2)), dma((2, 4, 2, 2)),
-            dma((2, 8)), dma((2,)), dma((2, 8)), dma((2,)), dma((2, 8)), dma((2, 8)),
-            dma((8,)), dma, dma((8,)), dma,
+            dma((3, 8)), dma((3,)), dma((3, 8)), dma((3,)), dma((3, 8)), dma((3, 8)),
+            dma((8,)), dma,
         ],
         compiler_params=pltpu.CompilerParams(
             collective_id=0, has_side_effects=True, vmem_limit_bytes=24 << 20
@@ -550,9 +591,10 @@
             first_upper = upper[:, :128]
         up_d[pair] = plain_digits(upper)
 
-    opan[0:16, :] = opan_ref[...]
     for k in range(16):
-        opan[16 + k:17 + k, :] = opan_ref[pl.ds(jnp.clip(tab[2, k], 0, 15), 1), :]
+        opan[k:k + 1, :] = opan_ref[k >> 1, (k & 1):(k & 1) + 1, :]
+        there = jnp.clip(tab[2, k], 0, 15)
+        opan[16 + k:17 + k, :] = opan_ref[there >> 1, pl.ds(there & 1, 1), :]
     old_low = centred(product(scaled_digits(opan[...]), uinv_d[...]))
     old_d = [scaled_digits(old_low[:16]), scaled_digits(old_low[16:])]
     for pair in range(8):

time: 45.4 us -> 44 us (0.969); the launches traced: 45.2 us -> 43.1 us
  Pallas kernels: 44.1 us -> 42 us
    pallas_call x1, Pallas kernels: 39.5 us -> 37.4 us  [exchange(): pl.pallas_call(exchange_kernel, name='exchange', out_shape=(pltpu.VMEM((2...]
where the time goes in v5:
time: 44 us; the launch traced here: 43.1 us
  Pallas kernels  42 us (95%)
  between operations  0.84 us (2%)
    pallas_call x1, Pallas kernels, exchange(): pl.pallas_call(exchange_kernel, name='exchange', out_shape=(pltpu.VMEM((2...  37.4 us
    pallas_call x1, Pallas kernels, update(): pl.pallas_call(update_kernel, name='update', out_shape=jax.ShapeDtypeStru...  4.64 us

profile of v5, /device:TPU:5, one launch (start us, length us, event | category | flops | bytes accessed | tf_op | source)
XLA Modules:
  0.0 43.1 jit_solution(2975578312282242704)
XLA Ops:
  0.0 0.0 copy-start.7
  0.0 0.0 copy-start.8
  0.0 37.4 %exchange.1 = (f32[2,8,128,128]{3,2,1,0:T(8,128)S(1)}, f32[2,16,8,128]{3,2,1,0:T(8,128)S(1)}, f32[8,8,128]{2,1,0:T(8,128)}, f32[256,128]{1,0:T(8,128)}, bf16[2,2...) custom-call(s32[1,128]{1,0:T(1,128)} %bitcast.35, ...), custom_call_target="tpu_custom_call" | custom-call | tf_op jit(solution)/shard_map/exchange/pallas_call | solution.py:533
  38.0 0.0 copy-done.7
  38.1 0.0 copy-done.8
  38.1 4.9 %conditional.1 = (f32[2,128,16,128]{3,2,1,0:T(8,128)}) conditional(s32[]{:T(128)} %bitcast.7, (f32[2,128,16,128]{3,2,1,0:T(8,128)}, s32[128]{0:T(128)S(1)}, s32[128]{0:T(128)S(1)}, s32[128,128]{1,0:T(8,128)}, s32[128,128]{1,0:T(8,128)}) %tuple.53, (s32[128]{0:T(128)S(1)}, s32[3,16]{1,0:T(4,128)}, f32[2,8,128,128]{3,2,1,0:T(8,128)S(1)}, ...), branch_computations={%region_0.3_spmd, %region_3.4_spmd} | conditional | flops 867625216 | bytes 175200640 | solution.py:671
  38.3 4.6 %update.1 = f32[256,2,8,128]{3,2,1,0:T(8,128)} custom-call(s32[3,16]{1,0:T(4,128)} %get-tuple-element.79.tab, f32[2,8,128,128]{3,2,1,0:T(8,128)S(1)} %get-tuple-element.80.new_ref, f32[2,16,8,128]{3,2,1,0:T(8,128)S(1)} %get-tuple-element.81.old_ref, f32[8,8,128]{2,1,0:T(8,128)} %get-tuple-element.82.opan_ref, f32[256,128]{1,0:T(8,128)} %get-tuple-element.83.low_ref, ...), custom_call_target="tpu_custom_call" | custom-call | tf_op jit(solution)/shard_map/cond/branch_1_fun/update/pallas_call | solution.py:650
Async XLA Ops:
  0.0 38.1 %copy-start.7 = (s32[128]{0:T(128)S(1)}, s32[128]{0:T(128)}, u32[]{:S(2)}) copy-start(s32[128]{0:T(128)} %param.15) | copy-start | bytes 1540
  0.0 38.1 %copy-start.8 = (s32[128]{0:T(128)S(1)}, s32[128]{0:T(128)}, u32[]{:S(2)}) copy-start(s32[128]{0:T(128)} %param.14) | copy-start | bytes 1540

commit v6 on v5

--- a/solution.py
+++ b/solution.py
@@ -582,14 +582,20 @@
     def reduced(x):
         return x - PF * jnp.floor((x + 0.5) * INV)
 
-    first_upper = None
-    for pair in range(8):
+    def make_upper(pair):
         c, e = pair // 4, (pair % 4) * 2
         x = jnp.concatenate([new_ref[c, e], new_ref[c, e + 1]], axis=1)
         upper = centred(product(linv_d[c], plain_digits(x)))
-        if pair == 0:
-            first_upper = upper[:, :128]
         up_d[pair] = plain_digits(upper)
+        return upper
+
+    def finish(pair, half, change):
+        for side in range(2):
+            e = 2 * pair + side
+            value = mat[e, 128 * half:128 * half + 128, :]
+            out2d[pl.ds(2048 * half + e, 128, stride=16), :] = reduced(
+                value - change[:, 128 * side:128 * side + 128]
+            )
 
     for k in range(16):
         opan[k:k + 1, :] = opan_ref[k >> 1, (k & 1):(k & 1) + 1, :]
@@ -597,7 +603,8 @@
         opan[16 + k:17 + k, :] = opan_ref[there >> 1, pl.ds(there & 1, 1), :]
     old_low = centred(product(scaled_digits(opan[...]), uinv_d[...]))
     old_d = [scaled_digits(old_low[:16]), scaled_digits(old_low[16:])]
-    for pair in range(8):
+
+    def displaced(pair):
         c = pair // 4
         change = product(old_d[c], up_d[pair])
         for side in range(2):
@@ -608,39 +615,44 @@
                 value = jnp.where(col == 0, positive(old_low[:16]), value)
             late2d[pl.ds(128 * c + e, 16, stride=8), :] = value
 
+    first_upper = make_upper(0)[:, :128]
+    for pair in range(1, 4):
+        make_upper(pair)
+    for pair in range(4):
+        make_upper(4 + pair)
+        displaced(pair)
+        for half in range(2):
+            finish(pair, half, product(low_d[half], up_d[pair]))
+    for pair in range(4, 8):
+        displaced(pair)
+
+    @pl.when(col == 0)
+    def _():
+        out2d[pl.ds(0, 256, stride=16), :] = positive(low_ref[...])
+
+        @pl.when(rank == 0)
+        def _():
+            sub = lax.broadcasted_iota(I32, (128, 128), 0)
+            order_hot = (sub == order_ref[...]).astype(BF16)
+            out2d[pl.ds(0, 128, stride=16), :] = one_hot_columns(positive(first_upper), order_hot)
+
     sent = []
+
+    def send(half, c):
+        for k in range(16):
+            slot = tab[c, k]
+            out[jnp.where((slot >> 7) == half, slot, 256), c] = late[c, k]
+        where = (pl.ds(128 * half, 128), c)
+        d = pltpu.make_async_copy(out.at[where], out_hbm.at[where], out_sem.at[half, c])
+        d.start()
+        sent.append(d)
+
+    send(0, 0)
+    send(1, 0)
     for half in range(2):
-        for pair in range(8):
-            c = pair // 4
-            change = product(low_d[half], up_d[pair])
-            for side in range(2):
-                e = 2 * pair + side
-                value = mat[e, 128 * half:128 * half + 128, :]
-                out2d[pl.ds(2048 * half + e, 128, stride=16), :] = reduced(
-                    value - change[:, 128 * side:128 * side + 128]
-                )
-            if pair == 0:
-                @pl.when(col == 0)
-                def _():
-                    part = low_ref[128 * half:128 * half + 128, :]
-                    out2d[pl.ds(2048 * half, 128, stride=16), :] = positive(part)
-
-                if half == 0:
-                    @pl.when((col == 0) & (rank == 0))
-                    def _():
-                        sub = lax.broadcasted_iota(I32, (128, 128), 0)
-                        order_hot = (sub == order_ref[...]).astype(BF16)
-                        out2d[pl.ds(0, 128, stride=16), :] = one_hot_columns(
-                            positive(first_upper), order_hot
-                        )
-            if pair % 4 == 3:
-                for k in range(16):
-                    slot = tab[c, k]
-                    out[jnp.where((slot >> 7) == half, slot, 256), c] = late[c, k]
-                where = (pl.ds(128 * half, 128), c)
-                d = pltpu.make_async_copy(out.at[where], out_hbm.at[where], out_sem.at[half, c])
-                d.start()
-                sent.append(d)
+        for pair in range(4, 8):
+            finish(pair, half, product(low_d[half], up_d[pair]))
+        send(half, 1)
     for d in sent:
         d.wait()
 

time: 44 us -> 43.7 us (level)
  no operation moved by 1% of the time
where the time goes in v6:
time: 43.7 us; the launch traced here: 42.9 us
  Pallas kernels  41.8 us (96%)
  between operations  0.84 us (2%)
    pallas_call x1, Pallas kernels, exchange(): pl.pallas_call(exchange_kernel, name='exchange', out_shape=(pltpu.VMEM((2...  37.4 us
    pallas_call x1, Pallas kernels, update(): pl.pallas_call(update_kernel, name='update', out_shape=jax.ShapeDtypeStru...  4.4 us

profile of v6, /device:TPU:5, one launch (start us, length us, event | category | flops | bytes accessed | tf_op | source)
XLA Modules:
  0.0 42.9 jit_solution(11108210973188019851)
XLA Ops:
  0.0 0.0 copy-start.7
  0.0 0.0 copy-start.8
  0.0 37.4 %exchange.1 = (f32[2,8,128,128]{3,2,1,0:T(8,128)S(1)}, f32[2,16,8,128]{3,2,1,0:T(8,128)S(1)}, f32[8,8,128]{2,1,0:T(8,128)}, f32[256,128]{1,0:T(8,128)}, bf16[2,2...) custom-call(s32[1,128]{1,0:T(1,128)} %bitcast.35, ...), custom_call_target="tpu_custom_call" | custom-call | tf_op jit(solution)/shard_map/exchange/pallas_call | solution.py:533
  38.0 0.0 copy-done.7
  38.1 0.0 copy-done.8
  38.1 4.6 %conditional.1 = (f32[2,128,16,128]{3,2,1,0:T(8,128)}) conditional(s32[]{:T(128)} %bitcast.7, (f32[2,128,16,128]{3,2,1,0:T(8,128)}, s32[128]{0:T(128)S(1)}, s32[128]{0:T(128)S(1)}, s32[128,128]{1,0:T(8,128)}, s32[128,128]{1,0:T(8,128)}) %tuple.53, (s32[128]{0:T(128)S(1)}, s32[3,16]{1,0:T(4,128)}, f32[2,8,128,128]{3,2,1,0:T(8,128)S(1)}, ...), branch_computations={%region_0.3_spmd, %region_3.4_spmd} | conditional | flops 867625216 | bytes 175200640 | solution.py:683
  38.3 4.4 %update.1 = f32[256,2,8,128]{3,2,1,0:T(8,128)} custom-call(s32[3,16]{1,0:T(4,128)} %get-tuple-element.79.tab, f32[2,8,128,128]{3,2,1,0:T(8,128)S(1)} %get-tuple-element.80.new_ref, f32[2,16,8,128]{3,2,1,0:T(8,128)S(1)} %get-tuple-element.81.old_ref, f32[8,8,128]{2,1,0:T(8,128)} %get-tuple-element.82.opan_ref, f32[256,128]{1,0:T(8,128)} %get-tuple-element.83.low_ref, ...), custom_call_target="tpu_custom_call" | custom-call | tf_op jit(solution)/shard_map/cond/branch_1_fun/update/pallas_call | solution.py:662
Async XLA Ops:
  0.0 38.1 %copy-start.7 = (s32[128]{0:T(128)S(1)}, s32[128]{0:T(128)}, u32[]{:S(2)}) copy-start(s32[128]{0:T(128)} %param.15) | copy-start | bytes 1540
  0.0 38.1 %copy-start.8 = (s32[128]{0:T(128)S(1)}, s32[128]{0:T(128)}, u32[]{:S(2)}) copy-start(s32[128]{0:T(128)} %param.14) | copy-start | bytes 1540
